TPU v7x, 32 devices: a whole 2x2x4 slice. The times are simulated.
32 devices in a mesh: mem: 2 (over x), lat: 4 (over z), lon: 4 (over y, core).
Axes of the slice: x: 2, y: 2, z: 4, core: 2. Of those that a mesh axis runs over, the one named last changes fastest.
Arguments:
- control: bfloat16 [8, 256, 128, 128], P('mem', 'lat', 'lon'), may hold values from -21 to 21
- ensemble: bfloat16 [8, 256, 128, 128], P('mem', 'lat', 'lon'), may hold values from -3 to 3
- precision: float32 [256, 128, 128], P('lat', 'lon'), may hold values from 0.5 to 8
- lat_taps: float32 [9], replicated, may hold values from 0.05 to 0.3
- lon_taps: float32 [9], replicated, may hold values from 0.05 to 0.3
- vertical: bfloat16 [128, 128], replicated, may hold values from -0.5 to 0.5
Outputs:
- hessian: float32 [8, 256, 128, 128], P('mem', 'lat', 'lon')
- curvature: float32 [], replicated
All inputs are finite; a program needn't handle non-finite values.
Results may differ from a plain program's by a relative error of at most 0.0038.
Values may be sent and summed in bfloat16 or wider, within the bound.
A program may use at most 64 MiB of HBM per device.

v0:
```python
import functools

import jax
import jax.numpy as jnp
from jax import lax
from jax.experimental import pallas as pl
from jax.experimental.pallas import tpu as pltpu
from jax.sharding import PartitionSpec as P

F32 = jnp.float32
BF16 = jnp.bfloat16
HALF = 4


def iota(shape, dim):
    return lax.broadcasted_iota(jnp.int32, shape, dim)


def filter_matrix(lat_taps, lon_taps, cols, reverse):
    taps = lat_taps.shape[0]
    shape = (HALF * cols, 3 * HALF * cols + 6 * HALF * HALF)
    out, src = iota(shape, 0), iota(shape, 1)
    main = 3 * HALF * cols
    side = 3 * HALF * HALF
    inside = src < main
    left = src < main + side
    packed = jnp.where(left, src - main, src - main - side)
    row = jnp.where(inside, src // cols, packed // HALF)
    col = jnp.where(
        inside, src % cols, packed % HALF + jnp.where(left, -HALF, cols)
    )
    down = row - out // cols
    across = col - out % cols + HALF
    first = jnp.zeros(shape, F32)
    second = jnp.zeros(shape, F32)
    for tap in range(taps):
        at = taps - 1 - tap if reverse else tap
        first = jnp.where(down == tap, lat_taps[at], first)
        second = jnp.where(across == tap, lon_taps[at], second)
    full = first * second
    high = full.astype(BF16)
    low = (full - high.astype(F32)).astype(BF16)
    return jnp.concatenate([high, low], axis=0)


def pack_matrix(cols):
    size = HALF * HALF
    shape = (2 * size, HALF * cols)
    out, src = iota(shape, 0), iota(shape, 1)
    place = out % size
    col = place % HALF + jnp.where(out < size, 0, cols - HALF)
    wanted = (place // HALF) * cols + col
    return jnp.where(src == wanted, 1.0, 0.0).astype(BF16)


def dot(a, b):
    return jnp.dot(a, b, preferred_element_type=F32)


def kernel(
    axes, sizes, entries, chunks, lat_taps, lon_taps, control, ensemble, precision, vertical, hess, curv,
    ext, ext2, ens, prec, own, inc_out, inc_in, halo, halo2, stage, stage2,
    filt, filt2, picks, vert, vert2, vert2t, sums, cs0, cs1, cs2,
    local_sem, send_sem, recv_sem, side_send, side_recv, inc_send, inc_recv, cs_send, cs_recv,
):
    members, rows, cols, levels = control.shape
    groups = rows // HALF
    per = groups // chunks
    cells = HALF * cols
    width = 2 if members % 2 == 0 else 1
    me = {a: lax.axis_index(a) for a in axes}
    n = dict(zip(axes, sizes))

    def device(**at):
        return tuple(at.get(a, me[a]) for a in axes)

    lat, lon = me["lat"], me["lon"]
    left = lax.rem(lon + n["lon"] - 1, n["lon"])
    right = lax.rem(lon + 1, n["lon"])
    has_up = lat > 0
    has_down = lat < n["lat"] - 1

    loads = [
        pltpu.make_async_copy(control, ext.at[:, pl.ds(HALF, rows)], local_sem.at[0]),
        pltpu.make_async_copy(vertical, vert, local_sem.at[1]),
        pltpu.make_async_copy(ensemble, ens, local_sem.at[2]),
        pltpu.make_async_copy(precision, prec, local_sem.at[3]),
    ]
    for load in loads:
        load.start()

    barrier = pltpu.get_barrier_semaphore()
    fixed = 0
    for axis in axes:
        for step in range(1, n[axis]):
            to = device(**{axis: lax.rem(me[axis] + step, n[axis])})
            pl.semaphore_signal(barrier, inc=1, device_id=to, device_id_type=pl.DeviceIdType.MESH)
            fixed += 1
    for has, row in ((has_up, lat - 1), (has_down, lat + 1)):
        @pl.when(has)
        def _():
            for col in (left, right):
                pl.semaphore_signal(
                    barrier, inc=1, device_id=device(lat=row, lon=col), device_id_type=pl.DeviceIdType.MESH
                )
    corners = jnp.where(has_up, 2, 0) + jnp.where(has_down, 2, 0)
    pl.semaphore_wait(barrier, fixed + corners)

    def remote(src, dst, send, recv, to):
        return pltpu.make_async_remote_copy(
            src_ref=src, dst_ref=dst, send_sem=send, recv_sem=recv,
            device_id=to, device_id_type=pl.DeviceIdType.MESH,
        )

    def row_copies(phase, up_src, down_src, dst):
        up = remote(
            up_src, dst.at[:, pl.ds(rows + HALF, HALF)],
            send_sem.at[phase, 0], recv_sem.at[phase, 0], device(lat=lat - 1),
        )
        down = remote(
            down_src, dst.at[:, pl.ds(0, HALF)],
            send_sem.at[phase, 1], recv_sem.at[phase, 1], device(lat=lat + 1),
        )
        return [up], [down]

    def corner_copies(phase, src, dst):
        up, down = [], []
        for side, to in ((0, left), (1, right)):
            there = dst.at[1 - side]
            mine = src.at[side]
            up.append(remote(
                mine.at[:, 0], there.at[:, groups + 1],
                send_sem.at[phase, 2 + side], recv_sem.at[phase, 2 + side], device(lat=lat - 1, lon=to),
            ))
            down.append(remote(
                mine.at[:, groups - 1], there.at[:, 0],
                send_sem.at[phase, 4 + side], recv_sem.at[phase, 4 + side], device(lat=lat + 1, lon=to),
            ))
        return up, down

    def side_copies(phase, src, dst, chunk):
        return [
            remote(
                src.at[side, :, pl.ds(chunk * per, per)], dst.at[1 - side, :, pl.ds(chunk * per + 1, per)],
                side_send.at[phase, side, chunk], side_recv.at[phase, side, chunk], device(lon=to),
            )
            for side, to in ((0, left), (1, right))
        ]

    def inc_copies(chunk):
        at = pl.ds(chunk * per, per)
        return [
            remote(
                inc_out.at[at], inc_in.at[step - 1, at],
                inc_send.at[step - 1, chunk], inc_recv.at[step - 1, chunk],
                device(mem=lax.rem(me["mem"] + step, n["mem"])),
            )
            for step in range(1, n["mem"])
        ]

    def each(has, copies, act):
        @pl.when(has)
        def _():
            for copy in copies:
                getattr(copy, act)()

    row_up, row_down = row_copies(
        0, control.at[:, pl.ds(0, HALF)], control.at[:, pl.ds(rows - HALF, HALF)], ext
    )
    each(has_up, row_up, "start")
    each(has_down, row_down, "start")

    @pl.when(jnp.logical_not(has_up))
    def _():
        for one, two in ((ext, halo), (ext2, halo2)):
            one[:, 0:HALF] = jnp.zeros((members, HALF, cols, levels), BF16)
            for side in range(2):
                two[side, :, 0] = jnp.zeros((members, HALF * HALF, levels), BF16)

    @pl.when(jnp.logical_not(has_down))
    def _():
        for one, two in ((ext, halo), (ext2, halo2)):
            one[:, rows + HALF : rows + 2 * HALF] = jnp.zeros((members, HALF, cols, levels), BF16)
            for side in range(2):
                two[side, :, groups + 1] = jnp.zeros((members, HALF * HALF, levels), BF16)

    picks[...] = pack_matrix(cols)
    loads[0].wait()

    def pack(blocks, go, dst):
        packed = dot(picks[...], jnp.concatenate(blocks, axis=1)).astype(BF16)
        size = HALF * HALF
        for m in range(members):
            lanes = slice(m * levels, (m + 1) * levels)
            dst[0, m, go] = packed[:size, lanes]
            dst[1, m, go] = packed[size:, lanes]

    def pack_group(go, carry):
        at = pl.ds(HALF * (go + 1), HALF)
        pack([ext[m, at].reshape(cells, levels) for m in range(members)], go, stage)
        return carry

    lax.fori_loop(0, groups, pack_group, 0, unroll=2)
    corner_up, corner_down = corner_copies(0, stage, halo)
    each(has_up, corner_up, "start")
    each(has_down, corner_down, "start")
    for chunk in range(chunks):
        for copy in side_copies(0, stage, halo, chunk):
            copy.start()

    filt[...] = filter_matrix(lat_taps, lon_taps, cols, False)
    filt2[...] = filter_matrix(lat_taps, lon_taps, cols, True)
    loads[1].wait()
    v = vert[...].astype(F32)
    vt = v.T
    blank = jnp.zeros((levels, levels), F32)

    def diagonal(block):
        if width == 1:
            return block.astype(BF16)
        return jnp.concatenate(
            [jnp.concatenate([block, blank], axis=1), jnp.concatenate([blank, block], axis=1)], axis=0
        ).astype(BF16)

    vert2[...] = diagonal(v)
    vert2t[...] = diagonal(vt)
    sums[...] = jnp.zeros_like(sums)

    def tile_sum(x):
        return jnp.sum(x.reshape(-1, 8, levels), axis=0)

    def squares(go, carry):
        total = sums[...]
        for m in range(members):
            block = ext[m, pl.ds(HALF * (go + 1), HALF)].reshape(cells, levels).astype(F32)
            total = total + tile_sum(block * block)
        sums[...] = total
        return carry

    lax.fori_loop(0, groups, squares, 0)
    loads[2].wait()
    loads[3].wait()

    def smooth(source, sides, matrix, go, pair):
        blocks = []
        for m in pair:
            blocks.append(jnp.concatenate([
                source[m, pl.ds(HALF * go, 3 * HALF)].reshape(3 * cells, levels),
                sides[0, m, pl.ds(go, 3)].reshape(3 * HALF * HALF, levels),
                sides[1, m, pl.ds(go, 3)].reshape(3 * HALF * HALF, levels),
            ], axis=0))
        both = dot(matrix[...], jnp.concatenate(blocks, axis=1))
        return both[:cells] + both[cells:]

    pairs = [tuple(range(m, m + width)) for m in range(0, members, width)]

    def forward(chunk):
        places = [chunk * per + g for g in range(per)]
        smoothed = [[smooth(ext, halo, filt, go, pair).astype(BF16) for pair in pairs] for go in places]
        for go, held in zip(places, smoothed):
            total = None
            for pair, value in zip(pairs, held):
                level = dot(value, vert2[...])
                for j, m in enumerate(pair):
                    spread = ens[m, pl.ds(HALF * go, HALF)].reshape(cells, levels).astype(F32)
                    term = spread * level[:, j * levels : (j + 1) * levels]
                    total = term if total is None else total + term
            own[go] = total
            inc_out[go] = total.astype(BF16)

    peers = n["mem"] - 1

    def weigh(go):
        increment = own[go]
        for peer in range(peers):
            increment = increment + inc_in[peer, go].astype(F32)
        weighted = prec[pl.ds(HALF * go, HALF)].reshape(cells, levels) * increment
        sums[...] += tile_sum(weighted * increment) * (1.0 / n["mem"])
        own[go] = weighted

    def adjoint(go):
        weighted = own[go]
        blocks = []
        for pair in pairs:
            parts = []
            for m in pair:
                spread = ens[m, pl.ds(HALF * go, HALF)].reshape(cells, levels).astype(F32)
                parts.append((spread * weighted).astype(BF16))
            result = dot(jnp.concatenate(parts, axis=1), vert2t[...]).astype(BF16)
            for j, m in enumerate(pair):
                block = result[:, j * levels : (j + 1) * levels]
                ext2[m, pl.ds(HALF * (go + 1), HALF)] = block.reshape(HALF, cols, levels)
                blocks.append(block)
        pack(blocks, go, stage2)

    def final(go):
        for pair in pairs:
            back = smooth(ext2, halo2, filt2, go, pair)
            for j, m in enumerate(pair):
                held = ext[m, pl.ds(HALF * (go + 1), HALF)].astype(F32)
                block = back[:, j * levels : (j + 1) * levels].reshape(HALF, cols, levels)
                hess[m, pl.ds(HALF * go, HALF)] = held + block

    def of_chunk(work, chunk):
        for g in range(per):
            work(chunk * per + g)

    def wait_sides(phase, src, dst, chunk):
        for copy in side_copies(phase, src, dst, chunk):
            copy.wait_recv()

    def forward_chunk(chunk, carry):
        forward(chunk)
        for copy in inc_copies(chunk):
            copy.start()
        return carry

    def forward_wait(chunk, carry):
        wait_sides(0, stage, halo, chunk + 1)
        return forward_chunk(chunk, carry)

    each(has_up, row_down + corner_down, "wait_recv")
    each(has_down, row_up + corner_up, "wait_recv")
    wait_sides(0, stage, halo, 0)
    lax.fori_loop(0, chunks - 1, forward_wait, 0)
    forward_chunk(chunks - 1, 0)

    row2_up, row2_down = row_copies(
        1, ext2.at[:, pl.ds(HALF, HALF)], ext2.at[:, pl.ds(rows, HALF)], ext2
    )
    corner2_up, corner2_down = corner_copies(1, stage2, halo2)

    def weigh_chunk(chunk, carry):
        for copy in inc_copies(chunk):
            copy.wait_recv()
        of_chunk(weigh, chunk)
        return carry

    def weigh_adjoint(chunk, carry):
        weigh_chunk(chunk, carry)
        return adjoint_chunk(chunk, carry)

    def adjoint_chunk(chunk, carry):
        of_chunk(adjoint, chunk)
        each(jnp.logical_and(has_up, chunk == 0), row2_up + corner2_up, "start")
        each(jnp.logical_and(has_down, chunk == chunks - 1), row2_down + corner2_down, "start")
        for copy in side_copies(1, stage2, halo2, chunk):
            copy.start()
        return carry

    def final_chunk(chunk, carry):
        of_chunk(final, chunk)
        return carry

    def final_wait(chunk, carry):
        wait_sides(1, stage2, halo2, chunk + 1)
        return final_chunk(chunk, carry)

    lag = min(4, chunks - 2)

    def both_chunks(chunk, carry):
        adjoint_chunk(chunk, carry)
        return final_wait(chunk - lag, carry)

    bufs = (cs0, cs1, cs2)

    def reduce_copies(index):
        axis, buf = axes[index], bufs[index]
        mine = me[axis]
        out, arrive = [], []
        for step in range(1, n[axis]):
            other = lax.rem(mine + step, n[axis])
            to = device(**{axis: other})
            sem = cs_send.at[index, step - 1]
            out.append(remote(buf.at[mine], buf.at[mine], sem, cs_recv.at[index, mine], to))
            arrive.append(remote(buf.at[other], buf.at[other], sem, cs_recv.at[index, other], to))
        return out, arrive

    def reduce_start(index, partial):
        bufs[index][me[axes[index]]] = partial
        for copy in reduce_copies(index)[0]:
            copy.start()

    def reduce_end(index):
        out, arrive = reduce_copies(index)
        for copy in arrive:
            copy.wait_recv()
        for copy in out:
            copy.wait_send()
        partial = bufs[index][0]
        for other in range(1, n[axes[index]]):
            partial = partial + bufs[index][other]
        return partial

    lax.fori_loop(0, lag + 1, weigh_adjoint, 0)
    lax.fori_loop(lag + 1, chunks, weigh_chunk, 0)
    reduce_start(0, sums[...])
    wait_sides(1, stage2, halo2, 0)
    wait_sides(1, stage2, halo2, 1)
    lax.fori_loop(lag + 1, chunks, both_chunks, 0)
    reduce_start(1, reduce_end(0))
    rest = chunks - lag
    middle = rest + (lag - 1) // 2 + 1
    lax.fori_loop(rest, middle, final_wait, 0)
    reduce_start(2, reduce_end(1))
    lax.fori_loop(middle, chunks - 1, final_wait, 0)
    each(has_down, row2_up + corner2_up, "wait_recv")
    final_chunk(chunks - 1, 0)
    each(has_up, row2_down + corner2_down, "wait_recv")
    final_chunk(0, 0)
    curv[0, 0] = jnp.sum(reduce_end(2)) * (1.0 / entries)

    each(has_up, row_up + corner_up + row2_up + corner2_up, "wait_send")
    each(has_down, row_down + corner_down + row2_down + corner2_down, "wait_send")

    def finish(chunk, carry):
        for copy in side_copies(0, stage, halo, chunk) + side_copies(1, stage2, halo2, chunk):
            copy.wait_send()
        for copy in inc_copies(chunk):
            copy.wait_send()
        return carry

    lax.fori_loop(0, chunks, finish, 0)


def per_device(axes, sizes, control, ensemble, precision, lat_taps, lon_taps, vertical):
    members, rows, cols, levels = control.shape
    n = dict(zip(axes, sizes))
    groups = rows // HALF
    cells = HALF * cols
    pack = HALF * HALF
    entries = control.size
    for size in sizes:
        entries *= size
    chunks = next(c for c in (8, 4, groups) if groups % c == 0)
    width = 2 if members % 2 == 0 else 1
    inner = 3 * cells + 6 * pack
    smem = pl.BlockSpec(memory_space=pltpu.SMEM)
    anyspace = pl.BlockSpec(memory_space=pltpu.HBM)
    most = max(sizes)
    peers = max(n["mem"] - 1, 1)
    hessian, curvature = pl.pallas_call(
        functools.partial(kernel, axes, sizes, entries, chunks),
        out_shape=(
            pltpu.VMEM(control.shape, F32),
            jax.ShapeDtypeStruct((1, 1), F32),
        ),
        in_specs=[smem, smem, anyspace, anyspace, anyspace, anyspace],
        out_specs=(pl.BlockSpec(memory_space=pltpu.VMEM), smem),
        scratch_shapes=[
            pltpu.VMEM((members, rows + 2 * HALF, cols, levels), BF16),
            pltpu.VMEM((members, rows + 2 * HALF, cols, levels), BF16),
            pltpu.VMEM(control.shape, BF16),
            pltpu.VMEM(precision.shape, F32),
            pltpu.VMEM((groups, cells, levels), F32),
            pltpu.VMEM((groups, cells, levels), BF16),
            pltpu.VMEM((peers, groups, cells, levels), BF16),
            pltpu.VMEM((2, members, groups + 2, pack, levels), BF16),
            pltpu.VMEM((2, members, groups + 2, pack, levels), BF16),
            pltpu.VMEM((2, members, groups, pack, levels), BF16),
            pltpu.VMEM((2, members, groups, pack, levels), BF16),
            pltpu.VMEM((2 * cells, inner), BF16),
            pltpu.VMEM((2 * cells, inner), BF16),
            pltpu.VMEM((2 * pack, cells), BF16),
            pltpu.VMEM((levels, levels), BF16),
            pltpu.VMEM((width * levels, width * levels), BF16),
            pltpu.VMEM((width * levels, width * levels), BF16),
            pltpu.VMEM((8, levels), F32),
            pltpu.VMEM((sizes[0], 8, levels), F32),
            pltpu.VMEM((sizes[1], 8, levels), F32),
            pltpu.VMEM((sizes[2], 8, levels), F32),
            pltpu.SemaphoreType.DMA((4,)),
            pltpu.SemaphoreType.DMA((2, 6)),
            pltpu.SemaphoreType.DMA((2, 6)),
            pltpu.SemaphoreType.DMA((2, 2, chunks)),
            pltpu.SemaphoreType.DMA((2, 2, chunks)),
            pltpu.SemaphoreType.DMA((peers, chunks)),
            pltpu.SemaphoreType.DMA((peers, chunks)),
            pltpu.SemaphoreType.DMA((len(axes), most)),
            pltpu.SemaphoreType.DMA((len(axes), most)),
        ],
        compiler_params=pltpu.CompilerParams(
            collective_id=0, has_side_effects=True, vmem_limit_bytes=59 * 1024 * 1024
        ),
    )(lat_taps, lon_taps, control, ensemble, precision, vertical)
    return hessian, curvature.reshape(())


def solution(mesh):
    axes = tuple(mesh.axis_names)
    sizes = tuple(mesh.shape[a] for a in axes)
    in_specs = (
        P("mem", "lat", "lon", None),
        P("mem", "lat", "lon", None),
        P("lat", "lon", None),
        P(),
        P(),
        P(),
    )
    out_specs = (P("mem", "lat", "lon", None), P())
    return jax.shard_map(
        functools.partial(per_device, axes, sizes),
        mesh=mesh, in_specs=in_specs, out_specs=out_specs, check_vma=False,
    )
```

profile of v0, /device:TPU:0, one launch (start us, length us, event | category | flops | bytes accessed | tf_op | source)
XLA Modules:
  0.0 41.4 jit_solution(410624995709235055)
XLA Ops:
  0.6 37.0 %shard_map.77 = (f32[4,64,32,128]{3,2,1,0:T(8,128)S(1)}, f32[1,1]{1,0:T(1,128)}) custom-call(f32[9]{0:T(128)} %lat_taps.1, f32[9]{0:T(128)} %lon_taps.1, bf16[4,64,32,128]{3,2,1,0:T(8,128)(2,1)} %control.1, bf16[4,64,32,128]{3,2,1,0:T(8,128)(2,1)} %ensemble.1, f32[64,32,128]{2,1,0:T(8,128)} %precision.1, bf16[128,128]{1,0:T(8,128)(2,1)} %vertical.1), custom_call_target="tpu_custom_call" | custom-call | tf_op jit(solution)/shard_map/pallas_call | solution.py:442
  37.7 2.0 %copy.10 = f32[4,64,32,128]{3,2,1,0:T(8,128)} copy(f32[4,64,32,128]{3,2,1,0:T(8,128)S(1)} %get-tuple-element.6) | data formatting | bytes 8388608
where the time goes:
time: 41.6 us; the launch traced here: 41.4 us
  Pallas kernels  37 us (89%)
  between operations  2.33 us (6%)
  local copies, waits for them, and re-layouts  2.02 us (5%)
    pallas_call x1, Pallas kernels, per_device(): pl.pallas_call(functools.partial(kernel, axes, sizes, entries, chunks), o...  37 us
    unnamed x1, local copies, waits for them, and re-layouts  2.02 us

commit v1 on v0

v1 whole, which is shorter than its diff:
```python
import functools
import itertools
import math

import jax
import jax.numpy as jnp
from jax import lax
from jax.experimental import pallas as pl
from jax.experimental.pallas import tpu as pltpu
from jax.sharding import PartitionSpec as P

F32 = jnp.float32
BF16 = jnp.bfloat16
HALF = 4


def iota(shape, dim):
    return lax.broadcasted_iota(jnp.int32, shape, dim)


def filter_matrix(lat_taps, lon_taps, cols, reverse):
    taps = lat_taps.shape[0]
    shape = (HALF * cols, 3 * HALF * cols + 6 * HALF * HALF)
    out, src = iota(shape, 0), iota(shape, 1)
    main = 3 * HALF * cols
    side = 3 * HALF * HALF
    inside = src < main
    left = src < main + side
    packed = jnp.where(left, src - main, src - main - side)
    row = jnp.where(inside, src // cols, packed // HALF)
    col = jnp.where(
        inside, src % cols, packed % HALF + jnp.where(left, -HALF, cols)
    )
    down = row - out // cols
    across = col - out % cols + HALF
    first = jnp.zeros(shape, F32)
    second = jnp.zeros(shape, F32)
    for tap in range(taps):
        at = taps - 1 - tap if reverse else tap
        first = jnp.where(down == tap, lat_taps[at], first)
        second = jnp.where(across == tap, lon_taps[at], second)
    full = first * second
    high = full.astype(BF16)
    low = (full - high.astype(F32)).astype(BF16)
    return jnp.concatenate([high, low], axis=0)


def border_matrix(lat_taps, lon_taps, cols):
    taps = lat_taps.shape[0]
    tile = 2 * HALF
    side = 3 * HALF * HALF
    shape = (2 * tile * HALF, 2 * side)
    out, src = iota(shape, 0), iota(shape, 1)
    place = out % (2 * tile)
    left = src < side
    packed = jnp.where(left, src, src - side)
    down = packed // HALF - out // (2 * tile)
    col = packed % HALF + jnp.where(left, -HALF, cols)
    across = col - (place + jnp.where(place < tile, 0, cols - 2 * tile)) + HALF
    first = jnp.zeros(shape, F32)
    second = jnp.zeros(shape, F32)
    for tap in range(taps):
        first = jnp.where(down == tap, lat_taps[tap], first)
        second = jnp.where(across == tap, lon_taps[tap], second)
    full = first * second
    high = full.astype(BF16)
    low = (full - high.astype(F32)).astype(BF16)
    return jnp.concatenate([high, low], axis=0)


def dot(a, b):
    return jnp.dot(a, b, preferred_element_type=F32)


def kernel(
    axes, sizes, entries, chunks, lat_taps, lon_taps, control, ensemble, precision, vertical, hess, curv,
    ext, ext2, ens, prec, own_in, own_rim, wgt, inner_out, rim_out, inner_in, rim_in, keep, halo, halo2, stage, stage2,
    filt, filt2, border, vert, vert2, vert2t, sums, parts, taps1, taps2,
    local_sem, send_sem, recv_sem, side_send, side_recv, inc_send, inc_recv, part_send, part_recv,
):
    members, rows, cols, levels = control.shape
    groups = rows // HALF
    per = groups // chunks
    cells = HALF * cols
    width = 2 if members % 2 == 0 else 1
    me = {a: lax.axis_index(a) for a in axes}
    n = dict(zip(axes, sizes))

    def device(**at):
        return tuple(at.get(a, me[a]) for a in axes)

    def place(to):
        index = 0
        for size, at in zip(sizes, to):
            index = index * size + at
        return index

    lat, lon = me["lat"], me["lon"]
    left = lax.rem(lon + n["lon"] - 1, n["lon"])
    right = lax.rem(lon + 1, n["lon"])
    has_up = lat > 0
    has_down = lat < n["lat"] - 1
    steps = [s for s in itertools.product(*(range(size) for size in sizes)) if any(s)]

    def ahead(step):
        return tuple(lax.rem(me[a] + d, n[a]) if d else me[a] for a, d in zip(axes, step))

    loads = [
        pltpu.make_async_copy(control, ext.at[:, pl.ds(HALF, rows)], local_sem.at[0]),
        pltpu.make_async_copy(vertical, vert, local_sem.at[1]),
        pltpu.make_async_copy(ensemble, ens, local_sem.at[2]),
        pltpu.make_async_copy(precision, prec, local_sem.at[3]),
        pltpu.make_async_copy(lat_taps, taps1, local_sem.at[4]),
        pltpu.make_async_copy(lon_taps, taps2, local_sem.at[5]),
    ]
    for at in (4, 5, 0, 1, 2, 3):
        loads[at].start()

    barrier = pltpu.get_barrier_semaphore()
    for step in steps:
        pl.semaphore_signal(barrier, inc=1, device_id=ahead(step), device_id_type=pl.DeviceIdType.MESH)

    def remote(src, dst, send, recv, to):
        return pltpu.make_async_remote_copy(
            src_ref=src, dst_ref=dst, send_sem=send, recv_sem=recv,
            device_id=to, device_id_type=pl.DeviceIdType.MESH,
        )

    def row_copies(phase, up_src, down_src, dst):
        up = remote(
            up_src, dst.at[:, pl.ds(rows + HALF, HALF)],
            send_sem.at[phase, 0], recv_sem.at[phase, 0], device(lat=lat - 1),
        )
        down = remote(
            down_src, dst.at[:, pl.ds(0, HALF)],
            send_sem.at[phase, 1], recv_sem.at[phase, 1], device(lat=lat + 1),
        )
        return [up], [down]

    def corner_copies(phase, src, dst):
        up, down = [], []
        for side, to in ((0, left), (1, right)):
            there = dst.at[1 - side]
            mine = src.at[side]
            up.append(remote(
                mine.at[:, 0], there.at[:, groups + 1],
                send_sem.at[phase, 2 + side], recv_sem.at[phase, 2 + side], device(lat=lat - 1, lon=to),
            ))
            down.append(remote(
                mine.at[:, groups - 1], there.at[:, 0],
                send_sem.at[phase, 4 + side], recv_sem.at[phase, 4 + side], device(lat=lat + 1, lon=to),
            ))
        return up, down

    def side_copies(phase, src, dst, chunk):
        return [
            remote(
                src.at[side, :, pl.ds(chunk * per, per)], dst.at[1 - side, :, pl.ds(chunk * per + 1, per)],
                side_send.at[phase, side, chunk], side_recv.at[phase, side, chunk], device(lon=to),
            )
            for side, to in ((0, left), (1, right))
        ]

    def inc_copies(chunk, part):
        at = pl.ds(chunk * per, per)
        out, into = ((inner_out, inner_in), (rim_out, rim_in))[part]
        return [
            remote(
                out.at[at], into.at[step - 1, at],
                inc_send.at[part, step - 1, chunk], inc_recv.at[part, step - 1, chunk],
                device(mem=lax.rem(me["mem"] + step, n["mem"])),
            )
            for step in range(1, n["mem"])
        ]

    def each(has, copies, act):
        @pl.when(has)
        def _():
            for copy in copies:
                getattr(copy, act)()

    @pl.when(jnp.logical_not(has_up))
    def _():
        for one, two in ((ext, halo), (ext2, halo2)):
            one[:, 0:HALF] = jnp.zeros((members, HALF, cols, levels), BF16)
            for side in range(2):
                two[side, :, 0] = jnp.zeros((members, HALF * HALF, levels), BF16)

    @pl.when(jnp.logical_not(has_down))
    def _():
        for one, two in ((ext, halo), (ext2, halo2)):
            one[:, rows + HALF : rows + 2 * HALF] = jnp.zeros((members, HALF, cols, levels), BF16)
            for side in range(2):
                two[side, :, groups + 1] = jnp.zeros((members, HALF * HALF, levels), BF16)

    with jax.named_scope("taps"):
        loads[4].wait()
        loads[5].wait()
    with jax.named_scope("filt"):
        filt[...] = filter_matrix(taps1, taps2, cols, False)
        border[...] = border_matrix(taps1, taps2, cols)

    first = iota((2 * HALF, levels), 0) < HALF

    def edges(block):
        tile = 2 * HALF
        near = [block[cols * r : cols * r + tile] for r in range(HALF)]
        far = [block[cols * (r + 1) - tile : cols * (r + 1)] for r in range(HALF)]
        lefts = [jnp.where(first, near[r], pltpu.roll(near[r + 1], HALF, 0)) for r in range(0, HALF, 2)]
        rights = [jnp.where(first, pltpu.roll(far[r], HALF, 0), far[r + 1]) for r in range(0, HALF, 2)]
        return jnp.concatenate(lefts, axis=0).astype(BF16), jnp.concatenate(rights, axis=0).astype(BF16)

    def pack_group(go, carry):
        for m in range(members):
            block = ext[m, pl.ds(HALF * (go + 1), HALF)].reshape(cells, levels).astype(F32)
            stage[0, m, go], stage[1, m, go] = edges(block)
        return carry

    with jax.named_scope("load0"):
        loads[0].wait()
    with jax.named_scope("pack"):
        lax.fori_loop(0, groups, pack_group, 0, unroll=4)

    half = chunks // 2
    tile = 2 * HALF
    loads[1].wait()
    v = vert[...].astype(F32)
    vt = v.T
    blank = jnp.zeros((levels, levels), F32)

    def diagonal(block):
        if width == 1:
            return block.astype(BF16)
        return jnp.concatenate(
            [jnp.concatenate([block, blank], axis=1), jnp.concatenate([blank, block], axis=1)], axis=0
        ).astype(BF16)

    vert2[...] = diagonal(v)
    vert2t[...] = diagonal(vt)
    sums[...] = jnp.zeros_like(sums)

    def tile_sum(x):
        return jnp.sum(x.reshape(-1, 8, levels), axis=0)

    def squares(go, carry):
        total = sums[...]
        for m in range(members):
            block = ext[m, pl.ds(HALF * (go + 1), HALF)].reshape(cells, levels).astype(F32)
            total = total + tile_sum(block * block)
        sums[...] = total
        return carry

    def smooth(source, sides, matrix, go, pair):
        blocks = []
        for m in pair:
            blocks.append(jnp.concatenate([
                source[m, pl.ds(HALF * go, 3 * HALF)].reshape(3 * cells, levels),
                sides[0, m, pl.ds(go, 3)].reshape(3 * HALF * HALF, levels),
                sides[1, m, pl.ds(go, 3)].reshape(3 * HALF * HALF, levels),
            ], axis=0))
        both = dot(matrix[...], jnp.concatenate(blocks, axis=1))
        return both[:cells] + both[cells:]

    pairs = [tuple(range(m, m + width)) for m in range(0, members, width)]

    def inner_rows(x):
        return jnp.concatenate([x[cols * r + tile : cols * (r + 1) - tile] for r in range(HALF)], axis=0)

    def rim_rows(x):
        ends = []
        for r in range(HALF):
            ends += [x[cols * r : cols * r + tile], x[cols * (r + 1) - tile : cols * (r + 1)]]
        return jnp.concatenate(ends, axis=0)

    def merge_rows(inner, rim):
        span = cols - 2 * tile
        blocks = []
        for r in range(HALF):
            blocks += [
                rim[2 * tile * r : 2 * tile * r + tile], inner[span * r : span * (r + 1)],
                rim[2 * tile * r + tile : 2 * tile * (r + 1)],
            ]
        return jnp.concatenate(blocks, axis=0)

    def spread_of(m, go):
        return ens[m, pl.ds(HALF * go, HALF)].reshape(cells, levels).astype(F32)

    def contribute(chunk, smoothed, pick, own, out, part):
        leveled = dot(jnp.concatenate(smoothed, axis=0), vert2[...])
        size = leveled.shape[0] // len(smoothed)
        at = 0
        for g in range(per):
            go = chunk * per + g
            total = None
            for pair in pairs:
                level = leveled[at : at + size]
                at += size
                for j, m in enumerate(pair):
                    term = pick(spread_of(m, go)) * level[:, j * levels : (j + 1) * levels]
                    total = term if total is None else total + term
            own[go] = total
            out[go] = total.astype(BF16)

    def forward_inner(chunk):
        smoothed = []
        for g in range(per):
            go = chunk * per + g
            for k, pair in enumerate(pairs):
                data = [ext[m, pl.ds(HALF * go, 3 * HALF)].reshape(3 * cells, levels) for m in pair]
                both = dot(filt[:, : 3 * cells], jnp.concatenate(data, axis=1))
                value = both[:cells] + both[cells:]
                keep[go, k] = rim_rows(value)
                smoothed.append(inner_rows(value).astype(BF16))
        contribute(chunk, smoothed, inner_rows, own_in, inner_out, 0)

    def forward_rim(chunk):
        smoothed = []
        for g in range(per):
            go = chunk * per + g
            for k, pair in enumerate(pairs):
                data = [
                    jnp.concatenate([
                        halo[0, m, pl.ds(go, 3)].reshape(3 * HALF * HALF, levels),
                        halo[1, m, pl.ds(go, 3)].reshape(3 * HALF * HALF, levels),
                    ], axis=0)
                    for m in pair
                ]
                both = dot(border[...], jnp.concatenate(data, axis=1))
                size = both.shape[0] // 2
                smoothed.append((keep[go, k] + both[:size] + both[size:]).astype(BF16))
        contribute(chunk, smoothed, rim_rows, own_rim, rim_out, 1)

    peers = n["mem"] - 1

    def weigh(chunk):
        for g in range(per):
            go = chunk * per + g
            inner, rim = own_in[go], own_rim[go]
            for peer in range(peers):
                inner = inner + inner_in[peer, go].astype(F32)
                rim = rim + rim_in[peer, go].astype(F32)
            increment = merge_rows(inner, rim)
            weighted = prec[pl.ds(HALF * go, HALF)].reshape(cells, levels) * increment
            sums[...] += tile_sum(weighted * increment) * (1.0 / n["mem"])
            wgt[go] = weighted

    def adjoint(chunk):
        places = [chunk * per + g for g in range(per)]
        rows_of = []
        for go in places:
            weighted = wgt[go]
            for pair in pairs:
                parts_of = []
                for m in pair:
                    parts_of.append((spread_of(m, go) * weighted).astype(BF16))
                rows_of.append(jnp.concatenate(parts_of, axis=1))
        result = dot(jnp.concatenate(rows_of, axis=0), vert2t[...])
        at = 0
        for go in places:
            for pair in pairs:
                for j, m in enumerate(pair):
                    block = result[at : at + cells, j * levels : (j + 1) * levels]
                    ext2[m, pl.ds(HALF * (go + 1), HALF)] = block.astype(BF16).reshape(HALF, cols, levels)
                    stage2[0, m, go], stage2[1, m, go] = edges(block)
                at += cells
        for copy in side_copies(1, stage2, halo2, chunk):
            copy.start()

    def final(chunk):
        for g in range(per):
            go = chunk * per + g
            for pair in pairs:
                back = smooth(ext2, halo2, filt2, go, pair)
                for j, m in enumerate(pair):
                    held = ext[m, pl.ds(HALF * (go + 1), HALF)].astype(F32)
                    block = back[:, j * levels : (j + 1) * levels].reshape(HALF, cols, levels)
                    hess[m, pl.ds(HALF * go, HALF)] = held + block

    def wait_sides(phase, src, dst, chunk):
        for copy in side_copies(phase, src, dst, chunk):
            copy.wait_recv()

    row2_up, row2_down = row_copies(
        1, ext2.at[:, pl.ds(HALF, HALF)], ext2.at[:, pl.ds(rows, HALF)], ext2
    )
    corner2_up, corner2_down = corner_copies(1, stage2, halo2)

    def here(at):
        return parts.at[place(at)], part_recv.at[place(at)]

    mine = device()
    part_out = [
        remote(here(mine)[0], here(mine)[0], part_send.at[k], here(mine)[1], ahead(step))
        for k, step in enumerate(steps)
    ]
    part_in = [
        remote(here(ahead(step))[0], here(ahead(step))[0], part_send.at[k], here(ahead(step))[1], ahead(step))
        for k, step in enumerate(steps)
    ]

    seen = {0: set(), 1: set()}

    def need_sides(phase, chunk):
        for at in (chunk - 1, chunk, chunk + 1):
            if 0 <= at < chunks and at not in seen[phase]:
                seen[phase].add(at)
                wait_sides(phase, *((stage, halo) if phase == 0 else (stage2, halo2)), at)

    row_up, row_down = row_copies(
        0, control.at[:, pl.ds(0, HALF)], control.at[:, pl.ds(rows - HALF, HALF)], ext
    )
    corner_up, corner_down = corner_copies(0, stage, halo)

    def start_inc(chunk, part):
        for copy in inc_copies(chunk, part):
            copy.start()

    def do_inner(chunk):
        if chunk == 0:
            with jax.named_scope("rowwait"):
                each(has_up, row_down + corner_down, "wait_recv")
        if chunk == chunks - 1:
            with jax.named_scope("rowwait"):
                each(has_down, row_up + corner_up, "wait_recv")
        with jax.named_scope("inner"):
            forward_inner(chunk)

    def do_rim(chunk):
        with jax.named_scope("rimwait"):
            need_sides(0, chunk)
        with jax.named_scope("rim"):
            forward_rim(chunk)
            start_inc(chunk, 1)

    adjointed, finished = set(), set()

    def do_adjoint(chunk):
        with jax.named_scope("incwait"):
            for part in range(2):
                for copy in inc_copies(chunk, part):
                    copy.wait_recv()
        with jax.named_scope("weigh"):
            weigh(chunk)
        adjointed.add(chunk)
        if len(adjointed) == chunks:
            with jax.named_scope("part"):
                parts[place(mine)] = jnp.sum(sums[...], axis=0, keepdims=True)
                for copy in part_out:
                    copy.start()
        with jax.named_scope("adj"):
            adjoint(chunk)
            if chunk == 0:
                each(has_up, row2_up + corner2_up, "start")
            if chunk == chunks - 1:
                each(has_down, row2_down + corner2_down, "start")

    def do_final(chunk):
        finished.add(chunk)
        with jax.named_scope("bwait"):
            need_sides(1, chunk)
            if chunk == 0:
                each(has_up, row2_down + corner2_down, "wait_recv")
            if chunk == chunks - 1:
                each(has_down, row2_up + corner2_up, "wait_recv")
        with jax.named_scope("fin"):
            final(chunk)

    middle = list(range(1, chunks - 1))
    early, late = middle[: half], middle[half:]
    with jax.named_scope("loads"):
        loads[2].wait()
    do_inner(middle[0])
    with jax.named_scope("barrier"):
        pl.semaphore_wait(barrier, len(steps))
    start_inc(middle[0], 0)
    for chunk in range(chunks):
        for copy in side_copies(0, stage, halo, chunk):
            copy.start()
    each(has_up, row_up + corner_up, "start")
    each(has_down, row_down + corner_down, "start")
    for chunk in middle[1:]:
        do_inner(chunk)
        start_inc(chunk, 0)
    with jax.named_scope("filt2"):
        filt2[...] = filter_matrix(taps1, taps2, cols, True)
    with jax.named_scope("squares"):
        lax.fori_loop(0, groups, squares, 0, unroll=2)
    loads[3].wait()
    for chunk in early:
        do_rim(chunk)
    for chunk in (0, chunks - 1):
        do_inner(chunk)
        start_inc(chunk, 0)
        do_rim(chunk)
    order = [*early, 0, chunks - 1, *late]
    at = 0
    for chunk in late:
        do_adjoint(order[at])
        at += 1
        do_rim(chunk)
    for position, now in enumerate(order):
        if position < at:
            continue
        do_adjoint(now)
        settled = order[:position]
        todo = [
            c for c in middle if c not in finished and all(d in settled for d in (c - 1, c, c + 1))
        ]
        if position < chunks - 1 and position > half - 1 and todo:
            do_final(todo[0])
    for chunk in middle:
        if chunk not in finished:
            do_final(chunk)
    do_final(chunks - 1)
    do_final(0)

    with jax.named_scope("redend"):
        for copy in part_in:
            copy.wait_recv()
        curv[0, 0] = jnp.sum(parts[...]) * (1.0 / entries)

    with jax.named_scope("finish"):
        for copy in part_out:
            copy.wait_send()
        each(has_up, row_up + corner_up + row2_up + corner2_up, "wait_send")
        each(has_down, row_down + corner_down + row2_down + corner2_down, "wait_send")

        def finish(chunk, carry):
            for copy in side_copies(0, stage, halo, chunk) + side_copies(1, stage2, halo2, chunk):
                copy.wait_send()
            for copy in inc_copies(chunk, 0) + inc_copies(chunk, 1):
                copy.wait_send()
            return carry

        lax.fori_loop(0, chunks, finish, 0)


def per_device(axes, sizes, control, ensemble, precision, lat_taps, lon_taps, vertical):
    members, rows, cols, levels = control.shape
    n = dict(zip(axes, sizes))
    groups = rows // HALF
    cells = HALF * cols
    pack = HALF * HALF
    entries = control.size
    for size in sizes:
        entries *= size
    chunks = next(c for c in (8, 4, groups) if groups % c == 0)
    width = 2 if members % 2 == 0 else 1
    inner = 3 * cells + 6 * pack
    rim = 4 * pack
    smem = pl.BlockSpec(memory_space=pltpu.SMEM)
    anyspace = pl.BlockSpec(memory_space=pltpu.HBM)
    peers = max(n["mem"] - 1, 1)
    hessian, curvature = pl.pallas_call(
        functools.partial(kernel, axes, sizes, entries, chunks),
        out_shape=(
            pltpu.VMEM(control.shape, F32),
            jax.ShapeDtypeStruct((1, 1), F32),
        ),
        in_specs=[anyspace, anyspace, anyspace, anyspace, anyspace, anyspace],
        out_specs=(pl.BlockSpec(memory_space=pltpu.VMEM), smem),
        scratch_shapes=[
            pltpu.VMEM((members, rows + 2 * HALF, cols, levels), BF16),
            pltpu.VMEM((members, rows + 2 * HALF, cols, levels), BF16),
            pltpu.VMEM(control.shape, BF16),
            pltpu.VMEM(precision.shape, F32),
            pltpu.VMEM((groups, cells - rim, levels), F32),
            pltpu.VMEM((groups, rim, levels), F32),
            pltpu.VMEM((groups, cells, levels), F32),
            pltpu.VMEM((groups, cells - rim, levels), BF16),
            pltpu.VMEM((groups, rim, levels), BF16),
            pltpu.VMEM((peers, groups, cells - rim, levels), BF16),
            pltpu.VMEM((peers, groups, rim, levels), BF16),
            pltpu.VMEM((groups, members // width, rim, width * levels), F32),
            pltpu.VMEM((2, members, groups + 2, pack, levels), BF16),
            pltpu.VMEM((2, members, groups + 2, pack, levels), BF16),
            pltpu.VMEM((2, members, groups, pack, levels), BF16),
            pltpu.VMEM((2, members, groups, pack, levels), BF16),
            pltpu.VMEM((2 * cells, inner), BF16),
            pltpu.VMEM((2 * cells, inner), BF16),
            pltpu.VMEM((2 * rim, 6 * pack), BF16),
            pltpu.VMEM((levels, levels), BF16),
            pltpu.VMEM((width * levels, width * levels), BF16),
            pltpu.VMEM((width * levels, width * levels), BF16),
            pltpu.VMEM((8, levels), F32),
            pltpu.VMEM((math.prod(sizes), 1, levels), F32),
            pltpu.SMEM(lat_taps.shape, F32),
            pltpu.SMEM(lon_taps.shape, F32),
            pltpu.SemaphoreType.DMA((6,)),
            pltpu.SemaphoreType.DMA((2, 6)),
            pltpu.SemaphoreType.DMA((2, 6)),
            pltpu.SemaphoreType.DMA((2, 2, chunks)),
            pltpu.SemaphoreType.DMA((2, 2, chunks)),
            pltpu.SemaphoreType.DMA((2, peers, chunks)),
            pltpu.SemaphoreType.DMA((2, peers, chunks)),
            pltpu.SemaphoreType.DMA((math.prod(sizes),)),
            pltpu.SemaphoreType.DMA((math.prod(sizes),)),
        ],
        compiler_params=pltpu.CompilerParams(
            collective_id=0, has_side_effects=True, vmem_limit_bytes=59 * 1024 * 1024
        ),
    )(lat_taps, lon_taps, control, ensemble, precision, vertical)
    return hessian, curvature.reshape(())


def solution(mesh):
    axes = tuple(mesh.axis_names)
    sizes = tuple(mesh.shape[a] for a in axes)
    in_specs = (
        P("mem", "lat", "lon", None),
        P("mem", "lat", "lon", None),
        P("lat", "lon", None),
        P(),
        P(),
        P(),
    )
    out_specs = (P("mem", "lat", "lon", None), P())
    return jax.shard_map(
        functools.partial(per_device, axes, sizes),
        mesh=mesh, in_specs=in_specs, out_specs=out_specs, check_vma=False,
    )
```

time: 41.6 us -> 34.6 us (0.83)
  Pallas kernels: 37 us -> 29.9 us
    pallas_call x1, Pallas kernels: 37 us -> 29.9 us  [per_device(): pl.pallas_call(functools.partial(kernel, axes, sizes, entries, chunks), o...]
where the time goes in v1:
time: 34.6 us; the launch traced here: 34.2 us
  Pallas kernels  29.9 us (86%)
  between operations  2.33 us (7%)
  local copies, waits for them, and re-layouts  2.02 us (6%)
    pallas_call x1, Pallas kernels, per_device(): pl.pallas_call(functools.partial(kernel, axes, sizes, entries, chunks), o...  29.9 us
    unnamed x1, local copies, waits for them, and re-layouts  2.02 us

profile of v1, /device:TPU:0, one launch (start us, length us, event | category | flops | bytes accessed | tf_op | source)
XLA Modules:
  0.0 34.2 jit_solution(9338638945277078275)
XLA Ops:
  0.6 29.9 %shard_map.77 = (f32[4,64,32,128]{3,2,1,0:T(8,128)S(1)}, f32[1,1]{1,0:T(1,128)}) custom-call(f32[9]{0:T(128)} %lat_taps.1, f32[9]{0:T(128)} %lon_taps.1, bf16[4,64,32,128]{3,2,1,0:T(8,128)(2,1)} %control.1, bf16[4,64,32,128]{3,2,1,0:T(8,128)(2,1)} %ensemble.1, f32[64,32,128]{2,1,0:T(8,128)} %precision.1, bf16[128,128]{1,0:T(8,128)(2,1)} %vertical.1), custom_call_target="tpu_custom_call" | custom-call | tf_op jit(solution)/shard_map/pallas_call | solution.py:554
  30.5 2.0 %copy.10 = f32[4,64,32,128]{3,2,1,0:T(8,128)} copy(f32[4,64,32,128]{3,2,1,0:T(8,128)S(1)} %get-tuple-element.6) | data formatting | bytes 8388608

commit v2 on v1

v2 whole, which is shorter than its diff:
```python
import functools
import itertools
import math

import jax
import jax.numpy as jnp
from jax import lax
from jax.experimental import pallas as pl
from jax.experimental.pallas import tpu as pltpu
from jax.sharding import PartitionSpec as P

F32 = jnp.float32
BF16 = jnp.bfloat16
HALF = 4


def iota(shape, dim):
    return lax.broadcasted_iota(jnp.int32, shape, dim)


def tap_products(lat_taps, lon_taps, down, across, reverse):
    taps = lat_taps.shape[0]
    first = jnp.zeros(down.shape, F32)
    second = jnp.zeros(down.shape, F32)
    for tap in range(taps):
        at = taps - 1 - tap if reverse else tap
        first = jnp.where(down == tap, lat_taps[at], first)
        second = jnp.where(across == tap, lon_taps[at], second)
    full = first * second
    high = full.astype(BF16)
    low = (full - high.astype(F32)).astype(BF16)
    return jnp.concatenate([high, low], axis=0)


def full_matrix(lat_taps, lon_taps, cols, reverse):
    shape = (HALF * cols, 3 * HALF * cols + 6 * HALF * HALF)
    out, src = iota(shape, 0), iota(shape, 1)
    main = 3 * HALF * cols
    side = 3 * HALF * HALF
    inside = src < main
    left = src < main + side
    packed = jnp.where(left, src - main, src - main - side)
    row = jnp.where(inside, src // cols, packed // HALF)
    col = jnp.where(
        inside, src % cols, packed % HALF + jnp.where(left, -HALF, cols)
    )
    return tap_products(lat_taps, lon_taps, row - out // cols, col - out % cols + HALF, reverse)


def inner_matrix(lat_taps, lon_taps, cols, reverse):
    span = cols - 4 * HALF
    shape = (HALF * span, 3 * HALF * cols)
    out, src = iota(shape, 0), iota(shape, 1)
    down = src // cols - out // span
    across = src % cols - (out % span + 2 * HALF) + HALF
    return tap_products(lat_taps, lon_taps, down, across, reverse)


def rim_matrix(lat_taps, lon_taps, side, reverse):
    tile = 2 * HALF
    main = 3 * HALF * 2 * tile
    shape = (HALF * tile, main + 3 * HALF * HALF)
    out, src = iota(shape, 0), iota(shape, 1)
    inside = src < main
    packed = src - main
    row = jnp.where(inside, src // (2 * tile), packed // HALF)
    col = jnp.where(inside, src % (2 * tile), packed % HALF + (2 * tile if side else -HALF))
    down = row - out // tile
    across = col - (out % tile + (tile if side else 0)) + HALF
    return tap_products(lat_taps, lon_taps, down, across, reverse)


def dot(a, b):
    return jnp.dot(a, b, preferred_element_type=F32)


def kernel(
    axes, sizes, entries, chunks, lat_taps, lon_taps, control, ensemble, precision, vertical, hess, curv,
    ext, ext2, ens, prec, own_in, own_rim, wgt, inner_out, rim_out, inner_in, rim_in, halo, halo2, stage, stage2,
    mid, near, far, filt2, vert, vert2, vert2t, sums, parts, taps1, taps2,
    local_sem, row_send, row_recv, corner_send, corner_recv, side_send, side_recv, inc_send, inc_recv, part_sem, met,
):
    members, rows, cols, levels = control.shape
    groups = rows // HALF
    per = groups // chunks
    cells = HALF * cols
    width = 2 if members % 2 == 0 else 1
    me = {a: lax.axis_index(a) for a in axes}
    n = dict(zip(axes, sizes))

    def device(**at):
        return tuple(at.get(a, me[a]) for a in axes)

    def place(to):
        index = 0
        for size, at in zip(sizes, to):
            index = index * size + at
        return index

    lat, lon = me["lat"], me["lon"]
    left = lax.rem(lon + n["lon"] - 1, n["lon"])
    right = lax.rem(lon + 1, n["lon"])
    has_up = lat > 0
    has_down = lat < n["lat"] - 1
    steps = [s for s in itertools.product(*(range(size) for size in sizes)) if any(s)]

    def ahead(step):
        return tuple(lax.rem(me[a] + d, n[a]) if d else me[a] for a, d in zip(axes, step))

    deep = per * HALF
    head, tail = pl.ds(0, 3 * deep), pl.ds(3 * deep, rows - 3 * deep)
    front, back_rows = pl.ds(deep, deep), pl.ds(2 * deep, rows - 2 * deep)
    loads = [
        pltpu.make_async_copy(control.at[:, head], ext.at[:, pl.ds(HALF, 3 * deep)], local_sem.at[0]),
        pltpu.make_async_copy(vertical, vert, local_sem.at[1]),
        pltpu.make_async_copy(ensemble.at[:, front], ens.at[:, front], local_sem.at[2]),
        pltpu.make_async_copy(ensemble.at[:, back_rows], ens.at[:, back_rows], local_sem.at[3]),
        pltpu.make_async_copy(lat_taps, taps1, local_sem.at[4]),
        pltpu.make_async_copy(lon_taps, taps2, local_sem.at[5]),
        pltpu.make_async_copy(ensemble.at[:, pl.ds(0, deep)], ens.at[:, pl.ds(0, deep)], local_sem.at[6]),
        pltpu.make_async_copy(precision, prec, local_sem.at[7]),
        pltpu.make_async_copy(
            control.at[:, tail], ext.at[:, pl.ds(HALF + 3 * deep, rows - 3 * deep)], local_sem.at[8]
        ),
    ]
    for at in (4, 5, 0, 2, 1, 8, 3, 6, 7):
        loads[at].start()

    barrier = pltpu.get_barrier_semaphore()
    plane = [s for s in steps if not s[axes.index("lat")]]

    def signal(semaphore, to):
        pl.semaphore_signal(semaphore, inc=1, device_id=to, device_id_type=pl.DeviceIdType.MESH)

    for step in plane:
        signal(barrier, ahead(step))
    for has, row in ((has_up, lat - 1), (has_down, lat + 1)):
        @pl.when(has)
        def _():
            for col in (lon, left, right):
                signal(barrier, device(lat=row, lon=col))
    beside = jnp.where(has_up, 1, 0) + jnp.where(has_down, 1, 0)

    def hello(turn):
        for has, row in ((has_up, lat - 1), (has_down, lat + 1)):
            @pl.when(has)
            def _():
                signal(met.at[turn], device(lat=row))

    def hear(turn):
        pl.semaphore_wait(met.at[turn], beside)

    def remote(src, dst, send, recv, to):
        return pltpu.make_async_remote_copy(
            src_ref=src, dst_ref=dst, send_sem=send, recv_sem=recv,
            device_id=to, device_id_type=pl.DeviceIdType.MESH,
        )

    def row_copies(phase, up_src, down_src, dst):
        up = remote(
            up_src, dst.at[:, pl.ds(rows + HALF, HALF)],
            row_send.at[phase, 0], row_recv.at[phase, 0], device(lat=lat - 1),
        )
        down = remote(
            down_src, dst.at[:, pl.ds(0, HALF)],
            row_send.at[phase, 1], row_recv.at[phase, 1], device(lat=lat + 1),
        )
        return [up], [down]

    def corner_copies(phase, src, dst):
        up, down = [], []
        for side, to in ((0, left), (1, right)):
            there = dst.at[1 - side]
            mine = src.at[side]
            up.append(remote(
                mine.at[:, 0], there.at[:, groups + 1],
                corner_send.at[phase, 0], corner_recv.at[phase, 0], device(lat=lat - 1, lon=to),
            ))
            down.append(remote(
                mine.at[:, groups - 1], there.at[:, 0],
                corner_send.at[phase, 1], corner_recv.at[phase, 1], device(lat=lat + 1, lon=to),
            ))
        return up, down

    def corner_waits(phase, src, dst):
        up = remote(
            src.at[:, :, 0], dst.at[:, :, groups + 1],
            corner_send.at[phase, 0], corner_recv.at[phase, 0], device(lat=lat - 1, lon=left),
        )
        down = remote(
            src.at[:, :, groups - 1], dst.at[:, :, 0],
            corner_send.at[phase, 1], corner_recv.at[phase, 1], device(lat=lat + 1, lon=left),
        )
        return [up], [down]

    def side_copies(phase, src, dst, chunk):
        return [
            remote(
                src.at[side, :, pl.ds(chunk * per, per)], dst.at[1 - side, :, pl.ds(chunk * per + 1, per)],
                side_send.at[phase], side_recv.at[phase, chunk], device(lon=to),
            )
            for side, to in ((0, left), (1, right))
        ]

    def side_arrival(phase, src, dst, chunk):
        return remote(
            src.at[:, :, pl.ds(chunk * per, per)], dst.at[:, :, pl.ds(chunk * per + 1, per)],
            side_send.at[phase], side_recv.at[phase, chunk], device(lon=left),
        )

    def inc_copies(chunk, part):
        at = pl.ds(chunk * per, per)
        out, into = ((inner_out, inner_in), (rim_out, rim_in))[part]
        return [
            remote(
                out.at[at], into.at[step - 1, at],
                inc_send.at[part, step - 1], inc_recv.at[part, step - 1, chunk],
                device(mem=lax.rem(me["mem"] + step, n["mem"])),
            )
            for step in range(1, n["mem"])
        ]

    def each(has, copies, act):
        @pl.when(has)
        def _():
            for copy in copies:
                getattr(copy, act)()

    @pl.when(jnp.logical_not(has_up))
    def _():
        for one, two in ((ext, halo), (ext2, halo2)):
            one[:, 0:HALF] = jnp.zeros((members, HALF, cols, levels), BF16)
            for side in range(2):
                two[side, :, 0] = jnp.zeros((members, HALF * HALF, levels), BF16)

    @pl.when(jnp.logical_not(has_down))
    def _():
        for one, two in ((ext, halo), (ext2, halo2)):
            one[:, rows + HALF : rows + 2 * HALF] = jnp.zeros((members, HALF, cols, levels), BF16)
            for side in range(2):
                two[side, :, groups + 1] = jnp.zeros((members, HALF * HALF, levels), BF16)

    with jax.named_scope("taps"):
        loads[4].wait()
        loads[5].wait()
    with jax.named_scope("filt"):
        mid[...] = inner_matrix(taps1, taps2, cols, False)

    first = iota((2 * HALF, levels), 0) < HALF

    def edges(block):
        tile = 2 * HALF
        near = [block[cols * r : cols * r + tile] for r in range(HALF)]
        far = [block[cols * (r + 1) - tile : cols * (r + 1)] for r in range(HALF)]
        lefts = [jnp.where(first, near[r], pltpu.roll(near[r + 1], HALF, 0)) for r in range(0, HALF, 2)]
        rights = [jnp.where(first, pltpu.roll(far[r], HALF, 0), far[r + 1]) for r in range(0, HALF, 2)]
        return jnp.concatenate(lefts, axis=0).astype(BF16), jnp.concatenate(rights, axis=0).astype(BF16)

    def pack_group(go, carry):
        for m in range(members):
            block = ext[m, pl.ds(HALF * (go + 1), HALF)].reshape(cells, levels).astype(F32)
            stage[0, m, go], stage[1, m, go] = edges(block)
        return carry

    half = chunks // 2
    tile = 2 * HALF
    loads[1].wait()
    v = vert[...].astype(F32)
    vt = v.T
    blank = jnp.zeros((levels, levels), F32)

    def diagonal(block):
        if width == 1:
            return block.astype(BF16)
        return jnp.concatenate(
            [jnp.concatenate([block, blank], axis=1), jnp.concatenate([blank, block], axis=1)], axis=0
        ).astype(BF16)

    vert2[...] = diagonal(v)
    vert2t[...] = diagonal(vt)
    sums[...] = jnp.zeros_like(sums)

    def tile_sum(x):
        return jnp.sum(x.reshape(-1, 8, levels), axis=0)

    def squares(go, carry):
        total = sums[...]
        for m in range(members):
            block = ext[m, pl.ds(HALF * (go + 1), HALF)].reshape(cells, levels).astype(F32)
            total = total + tile_sum(block * block)
        sums[...] = total
        return carry

    def halves(matrix, data):
        both = dot(matrix[...], data)
        size = both.shape[0] // 2
        return both[:size] + both[size:]

    def smooth_inner(source, matrix, go, pair):
        data = [source[m, pl.ds(HALF * go, 3 * HALF)].reshape(3 * cells, levels) for m in pair]
        return halves(matrix, jnp.concatenate(data, axis=1))

    def smooth_rim(source, sides, matrices, go, pair):
        ends = []
        for side, matrix in enumerate(matrices):
            data = [
                jnp.concatenate([
                    source[m, pl.ds(HALF * go, 3 * HALF), (cols - 2 * tile) * side : (cols - 2 * tile) * side + 2 * tile]
                    .reshape(3 * HALF * 2 * tile, levels),
                    sides[side, m, pl.ds(go, 3)].reshape(3 * HALF * HALF, levels),
                ], axis=0)
                for m in pair
            ]
            ends.append(halves(matrix, jnp.concatenate(data, axis=1)))
        return jnp.concatenate(ends, axis=0)

    pairs = [tuple(range(m, m + width)) for m in range(0, members, width)]

    def inner_rows(x):
        return jnp.concatenate([x[cols * r + tile : cols * (r + 1) - tile] for r in range(HALF)], axis=0)

    def rim_rows(x):
        lefts = [x[cols * r : cols * r + tile] for r in range(HALF)]
        rights = [x[cols * (r + 1) - tile : cols * (r + 1)] for r in range(HALF)]
        return jnp.concatenate(lefts + rights, axis=0)

    def merge_rows(inner, rim):
        span = cols - 2 * tile
        blocks = []
        for r in range(HALF):
            blocks += [
                rim[tile * r : tile * (r + 1)], inner[span * r : span * (r + 1)],
                rim[tile * (HALF + r) : tile * (HALF + r + 1)],
            ]
        return jnp.concatenate(blocks, axis=0)

    def spread_of(m, go):
        return ens[m, pl.ds(HALF * go, HALF)].reshape(cells, levels).astype(F32)

    def contribute(places, smoothed, pick, own, out):
        leveled = dot(jnp.concatenate(smoothed, axis=0), vert2[...])
        size = leveled.shape[0] // len(smoothed)
        at = 0
        for go in places:
            total = None
            for pair in pairs:
                level = leveled[at : at + size]
                at += size
                for j, m in enumerate(pair):
                    term = pick(spread_of(m, go)) * level[:, j * levels : (j + 1) * levels]
                    total = term if total is None else total + term
            own[go] = total
            out[go] = total.astype(BF16)

    def places_of(chunk):
        return [chunk * per + g for g in range(per)]

    def forward_inner(chunk):
        places = places_of(chunk)
        smoothed = [smooth_inner(ext, mid, go, pair).astype(BF16) for go in places for pair in pairs]
        contribute(places, smoothed, inner_rows, own_in, inner_out)

    def forward_rim(some):
        places = [go for chunk in some for go in places_of(chunk)]
        smoothed = [smooth_rim(ext, halo, (near, far), go, pair).astype(BF16) for go in places for pair in pairs]
        contribute(places, smoothed, rim_rows, own_rim, rim_out)

    peers = n["mem"] - 1

    def weigh(chunk):
        for g in range(per):
            go = chunk * per + g
            inner, rim = own_in[go], own_rim[go]
            for peer in range(peers):
                inner = inner + inner_in[peer, go].astype(F32)
                rim = rim + rim_in[peer, go].astype(F32)
            increment = merge_rows(inner, rim)
            weighted = prec[pl.ds(HALF * go, HALF)].reshape(cells, levels) * increment
            sums[...] += tile_sum(weighted * increment) * (1.0 / n["mem"])
            wgt[go] = weighted

    def adjoint(chunk):
        places = [chunk * per + g for g in range(per)]
        rows_of = []
        for go in places:
            weighted = wgt[go]
            for pair in pairs:
                parts_of = []
                for m in pair:
                    parts_of.append((spread_of(m, go) * weighted).astype(BF16))
                rows_of.append(jnp.concatenate(parts_of, axis=1))
        result = dot(jnp.concatenate(rows_of, axis=0), vert2t[...])
        at = 0
        for go in places:
            for pair in pairs:
                for j, m in enumerate(pair):
                    block = result[at : at + cells, j * levels : (j + 1) * levels]
                    ext2[m, pl.ds(HALF * (go + 1), HALF)] = block.astype(BF16).reshape(HALF, cols, levels)
                    stage2[0, m, go], stage2[1, m, go] = edges(block)
                at += cells
        for copy in side_copies(1, stage2, halo2, chunk):
            copy.start()

    def smooth(source, sides, matrix, go, pair):
        data = [
            jnp.concatenate([
                source[m, pl.ds(HALF * go, 3 * HALF)].reshape(3 * cells, levels),
                sides[0, m, pl.ds(go, 3)].reshape(3 * HALF * HALF, levels),
                sides[1, m, pl.ds(go, 3)].reshape(3 * HALF * HALF, levels),
            ], axis=0)
            for m in pair
        ]
        return halves(matrix, jnp.concatenate(data, axis=1))

    def final(chunk):
        for go in places_of(chunk):
            for pair in pairs:
                back = smooth(ext2, halo2, filt2, go, pair)
                for j, m in enumerate(pair):
                    held = ext[m, pl.ds(HALF * (go + 1), HALF)].astype(F32)
                    block = back[:, j * levels : (j + 1) * levels].reshape(HALF, cols, levels)
                    hess[m, pl.ds(HALF * go, HALF)] = held + block

    def wait_sides(phase, src, dst, chunk):
        side_arrival(phase, src, dst, chunk).wait_recv()

    row2_up, row2_down = row_copies(
        1, ext2.at[:, pl.ds(HALF, HALF)], ext2.at[:, pl.ds(rows, HALF)], ext2
    )
    corner2_up, corner2_down = corner_copies(1, stage2, halo2)
    both2_up, both2_down = corner_waits(1, stage2, halo2)

    mine = place(device())
    part_out = [remote(parts.at[mine], parts.at[mine], part_sem.at[0], part_sem.at[1], ahead(step)) for step in steps]
    others = parts.at[pl.ds(0, len(steps))]
    part_all = remote(others, others, part_sem.at[0], part_sem.at[1], ahead(steps[0]))

    seen = {0: set(), 1: set()}

    def need_sides(phase, chunk):
        for at in (chunk - 1, chunk, chunk + 1):
            if 0 <= at < chunks and at not in seen[phase]:
                seen[phase].add(at)
                wait_sides(phase, *((stage, halo) if phase == 0 else (stage2, halo2)), at)

    row_up, row_down = row_copies(
        0, control.at[:, pl.ds(0, HALF)], control.at[:, pl.ds(rows - HALF, HALF)], ext
    )
    corner_up, corner_down = corner_copies(0, stage, halo)
    both_up, both_down = corner_waits(0, stage, halo)

    def start_inc(chunk, part):
        for copy in inc_copies(chunk, part):
            copy.start()

    def do_inner(chunk):
        if chunk == 0:
            with jax.named_scope("rowwait"):
                each(has_up, row_down + both_down, "wait_recv")
        if chunk == chunks - 1:
            with jax.named_scope("rowwait"):
                each(has_down, row_up + both_up, "wait_recv")
        with jax.named_scope("inner"):
            forward_inner(chunk)

    def do_rim(*some):
        with jax.named_scope("rimwait"):
            for chunk in some:
                need_sides(0, chunk)
        with jax.named_scope("rim"):
            forward_rim(some)
            for chunk in some:
                start_inc(chunk, 1)

    adjointed = set()

    def do_adjoint(chunk):
        with jax.named_scope("incwait"):
            for part in range(2):
                for copy in inc_copies(chunk, part):
                    copy.wait_recv()
        with jax.named_scope("weigh"):
            weigh(chunk)
        adjointed.add(chunk)
        if len(adjointed) == chunks:
            with jax.named_scope("part"):
                parts[mine] = jnp.sum(sums[...], axis=0, keepdims=True)
                for copy in part_out:
                    copy.start()
        with jax.named_scope("adj"):
            adjoint(chunk)
            if chunk == 0:
                each(has_up, row2_up + corner2_up, "start")
            if chunk == chunks - 1:
                each(has_down, row2_down + corner2_down, "start")

    def do_final(chunk):
        with jax.named_scope("bwait"):
            need_sides(1, chunk)
            if chunk == 0:
                each(has_up, row2_down + both2_down, "wait_recv")
            if chunk == chunks - 1:
                each(has_down, row2_up + both2_up, "wait_recv")
        with jax.named_scope("fin"):
            final(chunk)

    middle = list(range(1, chunks - 1))
    turns = n["lat"] - 1
    with jax.named_scope("load0"):
        loads[0].wait()
        loads[2].wait()
    do_inner(middle[0])
    with jax.named_scope("barrier"):
        pl.semaphore_wait(barrier, len(plane) + 3 * beside)
    start_inc(middle[0], 0)
    each(has_up, row_up, "start")
    each(has_down, row_down, "start")
    with jax.named_scope("load8"):
        loads[8].wait()
    with jax.named_scope("pack"):
        lax.fori_loop(0, groups, pack_group, 0, unroll=4)
    for chunk in range(chunks):
        for copy in side_copies(0, stage, halo, chunk):
            copy.start()
        if chunk == half:
            each(has_up, corner_up, "start")
            each(has_down, corner_down, "start")
    met_turns = []

    def meet():
        turn = len(met_turns)
        if turn > turns:
            return
        met_turns.append(turn)
        with jax.named_scope("meet"):
            if turn > 0:
                hear(turn - 1)
            if turn < turns:
                hello(turn)

    meet()
    with jax.named_scope("load3"):
        loads[3].wait()
        loads[6].wait()
    for chunk in middle[1:]:
        do_inner(chunk)
        start_inc(chunk, 0)
        if chunk == middle[half - 1]:
            meet()
    with jax.named_scope("filt2"):
        near[...] = rim_matrix(taps1, taps2, 0, False)
        far[...] = rim_matrix(taps1, taps2, 1, False)
        filt2[...] = full_matrix(taps1, taps2, cols, True)
    with jax.named_scope("squares"):
        lax.fori_loop(0, groups, squares, 0, unroll=2)
    with jax.named_scope("load7"):
        loads[7].wait()
    last = chunks - 1
    lead = middle[: half - 1]
    rest = [c for c in middle if c not in lead and c != last - 1]
    batches = [lead[:1], lead[1:], [0], *[[c] for c in rest], [last, last - 1]]
    order = [c for batch in batches for c in batch]
    at = 0
    for index, batch in enumerate(batches):
        if batch:
            do_rim(*batch)
        if index == 0:
            for chunk in (0, last):
                do_inner(chunk)
                start_inc(chunk, 0)
        if index == 1:
            meet()
        if index >= 2 and index % 2 == 0 and at < len(order) - 2:
            do_adjoint(order[at])
            at += 1
    for position, now in enumerate(order):
        if position < at:
            continue
        if position == chunks - 2:
            while len(met_turns) <= turns:
                meet()
        do_adjoint(now)
    for chunk in middle:
        do_final(chunk)
    do_final(last)
    do_final(0)

    with jax.named_scope("redend"):
        part_all.wait_recv()
        curv[0, 0] = jnp.sum(parts[...]) * (1.0 / entries)

    with jax.named_scope("finish"):
        part_all.wait_send()
        each(has_up, row_up + both_up + row2_up + both2_up, "wait_send")
        each(has_down, row_down + both_down + row2_down + both2_down, "wait_send")
        for phase, src, dst in ((0, stage, halo), (1, stage2, halo2)):
            remote(src, dst.at[:, :, pl.ds(1, groups)], side_send.at[phase], side_recv.at[phase, 0], device(lon=left)).wait_send()
        for part, out, into in ((0, inner_out, inner_in), (1, rim_out, rim_in)):
            for step in range(1, n["mem"]):
                remote(
                    out, into.at[step - 1], inc_send.at[part, step - 1], inc_recv.at[part, step - 1, 0],
                    device(mem=lax.rem(me["mem"] + step, n["mem"])),
                ).wait_send()


def per_device(axes, sizes, control, ensemble, precision, lat_taps, lon_taps, vertical):
    members, rows, cols, levels = control.shape
    n = dict(zip(axes, sizes))
    groups = rows // HALF
    cells = HALF * cols
    pack = HALF * HALF
    entries = control.size
    for size in sizes:
        entries *= size
    chunks = next(c for c in (8, 4, groups) if groups % c == 0)
    width = 2 if members % 2 == 0 else 1
    rim = 4 * pack
    smem = pl.BlockSpec(memory_space=pltpu.SMEM)
    anyspace = pl.BlockSpec(memory_space=pltpu.HBM)
    peers = max(n["mem"] - 1, 1)
    hessian, curvature = pl.pallas_call(
        functools.partial(kernel, axes, sizes, entries, chunks),
        out_shape=(
            pltpu.VMEM(control.shape, F32),
            jax.ShapeDtypeStruct((1, 1), F32),
        ),
        in_specs=[anyspace, anyspace, anyspace, anyspace, anyspace, anyspace],
        out_specs=(pl.BlockSpec(memory_space=pltpu.VMEM), smem),
        scratch_shapes=[
            pltpu.VMEM((members, rows + 2 * HALF, cols, levels), BF16),
            pltpu.VMEM((members, rows + 2 * HALF, cols, levels), BF16),
            pltpu.VMEM(control.shape, BF16),
            pltpu.VMEM(precision.shape, F32),
            pltpu.VMEM((groups, cells - rim, levels), F32),
            pltpu.VMEM((groups, rim, levels), F32),
            pltpu.VMEM((groups, cells, levels), F32),
            pltpu.VMEM((groups, cells - rim, levels), BF16),
            pltpu.VMEM((groups, rim, levels), BF16),
            pltpu.VMEM((peers, groups, cells - rim, levels), BF16),
            pltpu.VMEM((peers, groups, rim, levels), BF16),
            pltpu.VMEM((2, members, groups + 2, pack, levels), BF16),
            pltpu.VMEM((2, members, groups + 2, pack, levels), BF16),
            pltpu.VMEM((2, members, groups, pack, levels), BF16),
            pltpu.VMEM((2, members, groups, pack, levels), BF16),
            pltpu.VMEM((2 * (cells - rim), 3 * cells), BF16),
            pltpu.VMEM((rim, 15 * pack), BF16),
            pltpu.VMEM((rim, 15 * pack), BF16),
            pltpu.VMEM((2 * cells, 3 * cells + 6 * pack), BF16),
            pltpu.VMEM((levels, levels), BF16),
            pltpu.VMEM((width * levels, width * levels), BF16),
            pltpu.VMEM((width * levels, width * levels), BF16),
            pltpu.VMEM((8, levels), F32),
            pltpu.VMEM((math.prod(sizes), 1, levels), F32),
            pltpu.SMEM(lat_taps.shape, F32),
            pltpu.SMEM(lon_taps.shape, F32),
            pltpu.SemaphoreType.DMA((9,)),
            pltpu.SemaphoreType.DMA((2, 2)),
            pltpu.SemaphoreType.DMA((2, 2)),
            pltpu.SemaphoreType.DMA((2, 2)),
            pltpu.SemaphoreType.DMA((2, 2)),
            pltpu.SemaphoreType.DMA((2,)),
            pltpu.SemaphoreType.DMA((2, chunks)),
            pltpu.SemaphoreType.DMA((2, peers)),
            pltpu.SemaphoreType.DMA((2, peers, chunks)),
            pltpu.SemaphoreType.DMA((2,)),
            pltpu.SemaphoreType.REGULAR((max(n["lat"] - 1, 1),)),
        ],
        compiler_params=pltpu.CompilerParams(
            collective_id=0, has_side_effects=True, vmem_limit_bytes=59 * 1024 * 1024
        ),
    )(lat_taps, lon_taps, control, ensemble, precision, vertical)
    return hessian, curvature.reshape(())


def solution(mesh):
    axes = tuple(mesh.axis_names)
    sizes = tuple(mesh.shape[a] for a in axes)
    in_specs = (
        P("mem", "lat", "lon", None),
        P("mem", "lat", "lon", None),
        P("lat", "lon", None),
        P(),
        P(),
        P(),
    )
    out_specs = (P("mem", "lat", "lon", None), P())
    return jax.shard_map(
        functools.partial(per_device, axes, sizes),
        mesh=mesh, in_specs=in_specs, out_specs=out_specs, check_vma=False,
    )
```

time: 34.6 us -> 31.3 us (0.905)
  Pallas kernels: 29.9 us -> 26.8 us
    pallas_call x1, Pallas kernels: 29.9 us -> 26.8 us  [per_device(): pl.pallas_call(functools.partial(kernel, axes, sizes, entries, chunks), o...]
where the time goes in v2:
time: 31.3 us; the launch traced here: 31.1 us
  Pallas kernels  26.8 us (86%)
  between operations  2.33 us (7%)
  local copies, waits for them, and re-layouts  2.02 us (6%)
    pallas_call x1, Pallas kernels, per_device(): pl.pallas_call(functools.partial(kernel, axes, sizes, entries, chunks), o...  26.8 us
    unnamed x1, local copies, waits for them, and re-layouts  2.02 us

profile of v2, /device:TPU:0, one launch (start us, length us, event | category | flops | bytes accessed | tf_op | source)
XLA Modules:
  0.0 31.1 jit_solution(2896519246399860015)
XLA Ops:
  0.6 26.8 %shard_map.77 = (f32[4,64,32,128]{3,2,1,0:T(8,128)S(1)}, f32[1,1]{1,0:T(1,128)}) custom-call(f32[9]{0:T(128)} %lat_taps.1, f32[9]{0:T(128)} %lon_taps.1, bf16[4,64,32,128]{3,2,1,0:T(8,128)(2,1)} %control.1, bf16[4,64,32,128]{3,2,1,0:T(8,128)(2,1)} %ensemble.1, f32[64,32,128]{2,1,0:T(8,128)} %precision.1, bf16[128,128]{1,0:T(8,128)(2,1)} %vertical.1), custom_call_target="tpu_custom_call" | custom-call | tf_op jit(solution)/shard_map/pallas_call | solution.py:621
  27.4 2.0 %copy.10 = f32[4,64,32,128]{3,2,1,0:T(8,128)} copy(f32[4,64,32,128]{3,2,1,0:T(8,128)S(1)} %get-tuple-element.6) | data formatting | bytes 8388608

commit v3 on v2

--- a/solution.py
+++ b/solution.py
@@ -1,6 +1,5 @@
 import functools
 import itertools
-import math
 
 import jax
 import jax.numpy as jnp
@@ -76,9 +75,9 @@
 
 def kernel(
     axes, sizes, entries, chunks, lat_taps, lon_taps, control, ensemble, precision, vertical, hess, curv,
-    ext, ext2, ens, prec, own_in, own_rim, wgt, inner_out, rim_out, inner_in, rim_in, halo, halo2, stage, stage2,
-    mid, near, far, filt2, vert, vert2, vert2t, sums, parts, taps1, taps2,
-    local_sem, row_send, row_recv, corner_send, corner_recv, side_send, side_recv, inc_send, inc_recv, part_sem, met,
+    ext, ext2, ens, prec, wgt, inners, rims, halo, halo2, stage, stage2,
+    mid, near, far, filt2, vert, vert2, vert2t, sums, parts, norms, taps1, taps2,
+    local_sem, row_send, row_recv, corner_send, corner_recv, side_send, side_recv, inc_send, inc_recv, part_sem, norm_send, norm_recv, met,
 ):
     members, rows, cols, levels = control.shape
     groups = rows // HALF
@@ -193,32 +192,53 @@
         )
         return [up], [down]
 
-    def side_copies(phase, src, dst, chunk):
+    def piece(phase, k):
+        if phase == 1:
+            return k * per, per
+        if k == 0:
+            return 0, 1
+        if k == chunks:
+            return groups - per + 1, per - 1
+        return (k - 1) * per + 1, per
+
+    def side_copies(phase, src, dst, k):
+        at, size = piece(phase, k)
         return [
             remote(
-                src.at[side, :, pl.ds(chunk * per, per)], dst.at[1 - side, :, pl.ds(chunk * per + 1, per)],
-                side_send.at[phase], side_recv.at[phase, chunk], device(lon=to),
+                src.at[side, :, pl.ds(at, size)], dst.at[1 - side, :, pl.ds(at + 1, size)],
+                side_send.at[phase], side_recv.at[phase, k], device(lon=to),
             )
             for side, to in ((0, left), (1, right))
         ]
 
-    def side_arrival(phase, src, dst, chunk):
+    def side_arrival(phase, src, dst, k):
+        at, size = piece(phase, k)
         return remote(
-            src.at[:, :, pl.ds(chunk * per, per)], dst.at[:, :, pl.ds(chunk * per + 1, per)],
-            side_send.at[phase], side_recv.at[phase, chunk], device(lon=left),
+            src.at[:, :, pl.ds(at, size)], dst.at[:, :, pl.ds(at + 1, size)],
+            side_send.at[phase], side_recv.at[phase, k], device(lon=left),
         )
 
     def inc_copies(chunk, part):
         at = pl.ds(chunk * per, per)
-        out, into = ((inner_out, inner_in), (rim_out, rim_in))[part]
+        field = (inners, rims)[part].at[me["mem"], at]
         return [
             remote(
-                out.at[at], into.at[step - 1, at],
-                inc_send.at[part, step - 1], inc_recv.at[part, step - 1, chunk],
+                field, field, inc_send.at[part, step - 1], inc_recv.at[part, step - 1, chunk],
                 device(mem=lax.rem(me["mem"] + step, n["mem"])),
             )
             for step in range(1, n["mem"])
         ]
+
+    def inc_arrivals(chunk, part):
+        at = pl.ds(chunk * per, per)
+        arrivals = []
+        for step in range(1, n["mem"]):
+            peer = lax.rem(me["mem"] + n["mem"] - step, n["mem"])
+            field = (inners, rims)[part].at[peer, at]
+            arrivals.append(remote(
+                field, field, inc_send.at[part, step - 1], inc_recv.at[part, step - 1, chunk], device(mem=peer)
+            ))
+        return arrivals
 
     def each(has, copies, act):
         @pl.when(has)
@@ -283,13 +303,11 @@
     def tile_sum(x):
         return jnp.sum(x.reshape(-1, 8, levels), axis=0)
 
-    def squares(go, carry):
-        total = sums[...]
+    def squares(go, total):
         for m in range(members):
             block = ext[m, pl.ds(HALF * (go + 1), HALF)].reshape(cells, levels).astype(F32)
             total = total + tile_sum(block * block)
-        sums[...] = total
-        return carry
+        return total
 
     def halves(matrix, data):
         both = dot(matrix[...], data)
@@ -337,7 +355,7 @@
     def spread_of(m, go):
         return ens[m, pl.ds(HALF * go, HALF)].reshape(cells, levels).astype(F32)
 
-    def contribute(places, smoothed, pick, own, out):
+    def contribute(places, smoothed, pick, field):
         leveled = dot(jnp.concatenate(smoothed, axis=0), vert2[...])
         size = leveled.shape[0] // len(smoothed)
         at = 0
@@ -349,8 +367,7 @@
                 for j, m in enumerate(pair):
                     term = pick(spread_of(m, go)) * level[:, j * levels : (j + 1) * levels]
                     total = term if total is None else total + term
-            own[go] = total
-            out[go] = total.astype(BF16)
+            field[me["mem"], go] = total.astype(BF16)
 
     def places_of(chunk):
         return [chunk * per + g for g in range(per)]
@@ -358,25 +375,23 @@
     def forward_inner(chunk):
         places = places_of(chunk)
         smoothed = [smooth_inner(ext, mid, go, pair).astype(BF16) for go in places for pair in pairs]
-        contribute(places, smoothed, inner_rows, own_in, inner_out)
+        contribute(places, smoothed, inner_rows, inners)
 
     def forward_rim(some):
         places = [go for chunk in some for go in places_of(chunk)]
         smoothed = [smooth_rim(ext, halo, (near, far), go, pair).astype(BF16) for go in places for pair in pairs]
-        contribute(places, smoothed, rim_rows, own_rim, rim_out)
-
-    peers = n["mem"] - 1
+        contribute(places, smoothed, rim_rows, rims)
 
     def weigh(chunk):
         for g in range(per):
             go = chunk * per + g
-            inner, rim = own_in[go], own_rim[go]
-            for peer in range(peers):
-                inner = inner + inner_in[peer, go].astype(F32)
-                rim = rim + rim_in[peer, go].astype(F32)
+            inner, rim = inners[0, go].astype(F32), rims[0, go].astype(F32)
+            for peer in range(1, n["mem"]):
+                inner = inner + inners[peer, go].astype(F32)
+                rim = rim + rims[peer, go].astype(F32)
             increment = merge_rows(inner, rim)
             weighted = prec[pl.ds(HALF * go, HALF)].reshape(cells, levels) * increment
-            sums[...] += tile_sum(weighted * increment) * (1.0 / n["mem"])
+            sums[...] += tile_sum(weighted * increment)
             wgt[go] = weighted
 
     def adjoint(chunk):
@@ -430,21 +445,30 @@
     corner2_up, corner2_down = corner_copies(1, stage2, halo2)
     both2_up, both2_down = corner_waits(1, stage2, halo2)
 
-    mine = place(device())
-    part_out = [remote(parts.at[mine], parts.at[mine], part_sem.at[0], part_sem.at[1], ahead(step)) for step in steps]
-    others = parts.at[pl.ds(0, len(steps))]
+    across = [s for s in steps if not s[axes.index("mem")]]
+    mine = lat * n["lon"] + lon
+    part_out = [remote(parts.at[mine], parts.at[mine], part_sem.at[0], part_sem.at[1], ahead(step)) for step in across]
+    others = parts.at[pl.ds(0, max(len(across), 1))]
     part_all = remote(others, others, part_sem.at[0], part_sem.at[1], ahead(steps[0]))
+    norm = norms.at[me["mem"]]
+    norm_out, norm_in = [], []
+    for step in range(1, n["mem"]):
+        to = lax.rem(me["mem"] + step, n["mem"])
+        norm_out.append(remote(norm, norm, norm_send.at[step - 1], norm_recv.at[step - 1], device(mem=to)))
+        of = lax.rem(me["mem"] + n["mem"] - step, n["mem"])
+        norm_in.append(remote(norms.at[of], norms.at[of], norm_send.at[step - 1], norm_recv.at[step - 1], device(mem=of)))
 
     seen = {0: set(), 1: set()}
 
     def need_sides(phase, chunk):
-        for at in (chunk - 1, chunk, chunk + 1):
-            if 0 <= at < chunks and at not in seen[phase]:
-                seen[phase].add(at)
-                wait_sides(phase, *((stage, halo) if phase == 0 else (stage2, halo2)), at)
+        wanted = (chunk, chunk + 1) if phase == 0 else (chunk - 1, chunk, chunk + 1)
+        for k in wanted:
+            if 0 <= k < chunks + (phase == 0) and k not in seen[phase] and piece(phase, k)[1] > 0:
+                seen[phase].add(k)
+                wait_sides(phase, *((stage, halo) if phase == 0 else (stage2, halo2)), k)
 
     row_up, row_down = row_copies(
-        0, control.at[:, pl.ds(0, HALF)], control.at[:, pl.ds(rows - HALF, HALF)], ext
+        0, ext.at[:, pl.ds(HALF, HALF)], ext.at[:, pl.ds(rows, HALF)], ext
     )
     corner_up, corner_down = corner_copies(0, stage, halo)
     both_up, both_down = corner_waits(0, stage, halo)
@@ -456,10 +480,10 @@
     def do_inner(chunk):
         if chunk == 0:
             with jax.named_scope("rowwait"):
-                each(has_up, row_down + both_down, "wait_recv")
+                each(has_up, row_down, "wait_recv")
         if chunk == chunks - 1:
             with jax.named_scope("rowwait"):
-                each(has_down, row_up + both_up, "wait_recv")
+                each(has_down, row_up, "wait_recv")
         with jax.named_scope("inner"):
             forward_inner(chunk)
 
@@ -467,6 +491,10 @@
         with jax.named_scope("rimwait"):
             for chunk in some:
                 need_sides(0, chunk)
+                if chunk == 0:
+                    each(has_up, both_down, "wait_recv")
+                if chunk == chunks - 1:
+                    each(has_down, both_up, "wait_recv")
         with jax.named_scope("rim"):
             forward_rim(some)
             for chunk in some:
@@ -477,14 +505,19 @@
     def do_adjoint(chunk):
         with jax.named_scope("incwait"):
             for part in range(2):
-                for copy in inc_copies(chunk, part):
+                for copy in inc_arrivals(chunk, part):
                     copy.wait_recv()
         with jax.named_scope("weigh"):
             weigh(chunk)
         adjointed.add(chunk)
         if len(adjointed) == chunks:
             with jax.named_scope("part"):
-                parts[mine] = jnp.sum(sums[...], axis=0, keepdims=True)
+                for copy in norm_in:
+                    copy.wait_recv()
+                total = sums[...]
+                for peer in range(n["mem"]):
+                    total = total + norms[peer]
+                parts[mine] = jnp.sum(total, axis=0, keepdims=True)
                 for copy in part_out:
                     copy.start()
         with jax.named_scope("adj"):
@@ -514,15 +547,16 @@
         pl.semaphore_wait(barrier, len(plane) + 3 * beside)
     start_inc(middle[0], 0)
     each(has_up, row_up, "start")
-    each(has_down, row_down, "start")
     with jax.named_scope("load8"):
         loads[8].wait()
+    each(has_down, row_down, "start")
     with jax.named_scope("pack"):
         lax.fori_loop(0, groups, pack_group, 0, unroll=4)
-    for chunk in range(chunks):
-        for copy in side_copies(0, stage, halo, chunk):
-            copy.start()
-        if chunk == half:
+    for k in [*range(1, half + 1), 0, chunks - 1, chunks, *range(half + 1, chunks - 1)]:
+        if piece(0, k)[1] > 0:
+            for copy in side_copies(0, stage, halo, k):
+                copy.start()
+        if k == 0:
             each(has_up, corner_up, "start")
             each(has_down, corner_down, "start")
     met_turns = []
@@ -547,32 +581,40 @@
         start_inc(chunk, 0)
         if chunk == middle[half - 1]:
             meet()
-    with jax.named_scope("filt2"):
+    with jax.named_scope("filt1"):
         near[...] = rim_matrix(taps1, taps2, 0, False)
         far[...] = rim_matrix(taps1, taps2, 1, False)
-        filt2[...] = full_matrix(taps1, taps2, cols, True)
-    with jax.named_scope("squares"):
-        lax.fori_loop(0, groups, squares, 0, unroll=2)
     with jax.named_scope("load7"):
         loads[7].wait()
     last = chunks - 1
     lead = middle[: half - 1]
     rest = [c for c in middle if c not in lead and c != last - 1]
-    batches = [lead[:1], lead[1:], [0], *[[c] for c in rest], [last, last - 1]]
-    order = [c for batch in batches for c in batch]
-    at = 0
-    for index, batch in enumerate(batches):
-        if batch:
-            do_rim(*batch)
-        if index == 0:
-            for chunk in (0, last):
-                do_inner(chunk)
-                start_inc(chunk, 0)
-        if index == 1:
+    order = [*lead, 0, last, *rest, last - 1]
+
+    def do_end(chunk):
+        do_inner(chunk)
+        start_inc(chunk, 0)
+
+    for chunk in lead:
+        do_rim(chunk)
+        if chunk == lead[-1]:
             meet()
-        if index >= 2 and index % 2 == 0 and at < len(order) - 2:
-            do_adjoint(order[at])
-            at += 1
+    do_end(0)
+    do_rim(0)
+    do_end(last)
+    with jax.named_scope("filt2"):
+        filt2[...] = full_matrix(taps1, taps2, cols, True)
+    do_rim(last)
+    do_adjoint(order[0])
+    if rest:
+        do_rim(*rest)
+    do_adjoint(order[1])
+    do_rim(last - 1)
+    with jax.named_scope("squares"):
+        norms[me["mem"]] = lax.fori_loop(0, groups, squares, jnp.zeros((8, levels), F32), unroll=2)
+        for copy in norm_out:
+            copy.start()
+    at = 2
     for position, now in enumerate(order):
         if position < at:
             continue
@@ -580,26 +622,32 @@
             while len(met_turns) <= turns:
                 meet()
         do_adjoint(now)
-    for chunk in middle:
+    done = {c: max(order.index(d) for d in (c - 1, c, c + 1)) for c in middle}
+    for chunk in sorted(middle, key=lambda c: (done[c], c)):
         do_final(chunk)
     do_final(last)
     do_final(0)
 
     with jax.named_scope("redend"):
-        part_all.wait_recv()
+        if across:
+            part_all.wait_recv()
         curv[0, 0] = jnp.sum(parts[...]) * (1.0 / entries)
 
     with jax.named_scope("finish"):
-        part_all.wait_send()
+        if across:
+            part_all.wait_send()
+        for copy in norm_out:
+            copy.wait_send()
         each(has_up, row_up + both_up + row2_up + both2_up, "wait_send")
         each(has_down, row_down + both_down + row2_down + both2_down, "wait_send")
         for phase, src, dst in ((0, stage, halo), (1, stage2, halo2)):
             remote(src, dst.at[:, :, pl.ds(1, groups)], side_send.at[phase], side_recv.at[phase, 0], device(lon=left)).wait_send()
-        for part, out, into in ((0, inner_out, inner_in), (1, rim_out, rim_in)):
+        for part, field in ((0, inners), (1, rims)):
             for step in range(1, n["mem"]):
+                to = lax.rem(me["mem"] + step, n["mem"])
+                whole = field.at[me["mem"]]
                 remote(
-                    out, into.at[step - 1], inc_send.at[part, step - 1], inc_recv.at[part, step - 1, 0],
-                    device(mem=lax.rem(me["mem"] + step, n["mem"])),
+                    whole, whole, inc_send.at[part, step - 1], inc_recv.at[part, step - 1, 0], device(mem=to)
                 ).wait_send()
 
 
@@ -631,13 +679,9 @@
             pltpu.VMEM((members, rows + 2 * HALF, cols, levels), BF16),
             pltpu.VMEM(control.shape, BF16),
             pltpu.VMEM(precision.shape, F32),
-            pltpu.VMEM((groups, cells - rim, levels), F32),
-            pltpu.VMEM((groups, rim, levels), F32),
             pltpu.VMEM((groups, cells, levels), F32),
-            pltpu.VMEM((groups, cells - rim, levels), BF16),
-            pltpu.VMEM((groups, rim, levels), BF16),
-            pltpu.VMEM((peers, groups, cells - rim, levels), BF16),
-            pltpu.VMEM((peers, groups, rim, levels), BF16),
+            pltpu.VMEM((n["mem"], groups, cells - rim, levels), BF16),
+            pltpu.VMEM((n["mem"], groups, rim, levels), BF16),
             pltpu.VMEM((2, members, groups + 2, pack, levels), BF16),
             pltpu.VMEM((2, members, groups + 2, pack, levels), BF16),
             pltpu.VMEM((2, members, groups, pack, levels), BF16),
@@ -650,7 +694,8 @@
             pltpu.VMEM((width * levels, width * levels), BF16),
             pltpu.VMEM((width * levels, width * levels), BF16),
             pltpu.VMEM((8, levels), F32),
-            pltpu.VMEM((math.prod(sizes), 1, levels), F32),
+            pltpu.VMEM((n["lat"] * n["lon"], 1, levels), F32),
+            pltpu.VMEM((n["mem"], 8, levels), F32),
             pltpu.SMEM(lat_taps.shape, F32),
             pltpu.SMEM(lon_taps.shape, F32),
             pltpu.SemaphoreType.DMA((9,)),
@@ -659,10 +704,12 @@
             pltpu.SemaphoreType.DMA((2, 2)),
             pltpu.SemaphoreType.DMA((2, 2)),
             pltpu.SemaphoreType.DMA((2,)),
-            pltpu.SemaphoreType.DMA((2, chunks)),
+            pltpu.SemaphoreType.DMA((2, chunks + 1)),
             pltpu.SemaphoreType.DMA((2, peers)),
             pltpu.SemaphoreType.DMA((2, peers, chunks)),
             pltpu.SemaphoreType.DMA((2,)),
+            pltpu.SemaphoreType.DMA((peers,)),
+            pltpu.SemaphoreType.DMA((peers,)),
             pltpu.SemaphoreType.REGULAR((max(n["lat"] - 1, 1),)),
         ],
         compiler_params=pltpu.CompilerParams(

time: 31.3 us -> 29.6 us (0.946)
  Pallas kernels: 26.8 us -> 25.1 us
    pallas_call x1, Pallas kernels: 26.8 us -> 25.1 us  [per_device(): pl.pallas_call(functools.partial(kernel, axes, sizes, entries, chunks), o...]
where the time goes in v3:
time: 29.6 us; the launch traced here: 29.5 us
  Pallas kernels  25.1 us (85%)
  between operations  2.33 us (8%)
  local copies, waits for them, and re-layouts  2.02 us (7%)
    pallas_call x1, Pallas kernels, per_device(): pl.pallas_call(functools.partial(kernel, axes, sizes, entries, chunks), o...  25.1 us
    unnamed x1, local copies, waits for them, and re-layouts  2.02 us

profile of v3, /device:TPU:0, one launch (start us, length us, event | category | flops | bytes accessed | tf_op | source)
XLA Modules:
  0.0 29.5 jit_solution(4250303685444111014)
XLA Ops:
  0.6 25.1 %shard_map.77 = (f32[4,64,32,128]{3,2,1,0:T(8,128)S(1)}, f32[1,1]{1,0:T(1,128)}) custom-call(f32[9]{0:T(128)} %lat_taps.1, f32[9]{0:T(128)} %lon_taps.1, bf16[4,64,32,128]{3,2,1,0:T(8,128)(2,1)} %control.1, bf16[4,64,32,128]{3,2,1,0:T(8,128)(2,1)} %ensemble.1, f32[64,32,128]{2,1,0:T(8,128)} %precision.1, bf16[128,128]{1,0:T(8,128)(2,1)} %vertical.1), custom_call_target="tpu_custom_call" | custom-call | tf_op jit(solution)/shard_map/pallas_call | solution.py:669
  25.8 2.0 %copy.10 = f32[4,64,32,128]{3,2,1,0:T(8,128)} copy(f32[4,64,32,128]{3,2,1,0:T(8,128)S(1)} %get-tuple-element.6) | data formatting | bytes 8388608

commit v4 on v3

--- a/solution.py
+++ b/solution.py
@@ -107,10 +107,11 @@
         return tuple(lax.rem(me[a] + d, n[a]) if d else me[a] for a, d in zip(axes, step))
 
     deep = per * HALF
-    head, tail = pl.ds(0, 3 * deep), pl.ds(3 * deep, rows - 3 * deep)
+    first_rows = 2 * deep + HALF
+    head, tail = pl.ds(0, first_rows), pl.ds(first_rows, rows - first_rows)
     front, back_rows = pl.ds(deep, deep), pl.ds(2 * deep, rows - 2 * deep)
     loads = [
-        pltpu.make_async_copy(control.at[:, head], ext.at[:, pl.ds(HALF, 3 * deep)], local_sem.at[0]),
+        pltpu.make_async_copy(control.at[:, head], ext.at[:, pl.ds(HALF, first_rows)], local_sem.at[0]),
         pltpu.make_async_copy(vertical, vert, local_sem.at[1]),
         pltpu.make_async_copy(ensemble.at[:, front], ens.at[:, front], local_sem.at[2]),
         pltpu.make_async_copy(ensemble.at[:, back_rows], ens.at[:, back_rows], local_sem.at[3]),
@@ -119,10 +120,10 @@
         pltpu.make_async_copy(ensemble.at[:, pl.ds(0, deep)], ens.at[:, pl.ds(0, deep)], local_sem.at[6]),
         pltpu.make_async_copy(precision, prec, local_sem.at[7]),
         pltpu.make_async_copy(
-            control.at[:, tail], ext.at[:, pl.ds(HALF + 3 * deep, rows - 3 * deep)], local_sem.at[8]
+            control.at[:, tail], ext.at[:, pl.ds(HALF + first_rows, rows - first_rows)], local_sem.at[8]
         ),
     ]
-    for at in (4, 5, 0, 2, 1, 8, 3, 6, 7):
+    for at in (4, 5, 1, 0, 2, 8, 3, 6, 7):
         loads[at].start()
 
     barrier = pltpu.get_barrier_semaphore()
@@ -192,21 +193,26 @@
         )
         return [up], [down]
 
+    half = chunks // 2
+    sets = [[1, 2], *[[k] for k in range(3, half + 1)], [0], [chunks - 1, chunks], list(range(half + 1, chunks - 1))]
+    sets = [ks for ks in sets if ks]
+
     def piece(phase, k):
         if phase == 1:
             return k * per, per
-        if k == 0:
-            return 0, 1
-        if k == chunks:
-            return groups - per + 1, per - 1
-        return (k - 1) * per + 1, per
+        ks = sets[k]
+        start = max((ks[0] - 1) * per + 1, 0)
+        return start, min(ks[-1] * per + 1, groups) - start
+
+    def side_sem(phase, k):
+        return side_recv.at[phase * len(sets) + k]
 
     def side_copies(phase, src, dst, k):
         at, size = piece(phase, k)
         return [
             remote(
                 src.at[side, :, pl.ds(at, size)], dst.at[1 - side, :, pl.ds(at + 1, size)],
-                side_send.at[phase], side_recv.at[phase, k], device(lon=to),
+                side_send.at[phase], side_sem(phase, k), device(lon=to),
             )
             for side, to in ((0, left), (1, right))
         ]
@@ -215,30 +221,41 @@
         at, size = piece(phase, k)
         return remote(
             src.at[:, :, pl.ds(at, size)], dst.at[:, :, pl.ds(at + 1, size)],
-            side_send.at[phase], side_recv.at[phase, k], device(lon=left),
+            side_send.at[phase], side_sem(phase, k), device(lon=left),
         )
+
+    def inc_sem(chunk, part):
+        return chunk if part else chunks + (chunk == 0) + 2 * (chunk == chunks - 1)
 
     def inc_copies(chunk, part):
         at = pl.ds(chunk * per, per)
         field = (inners, rims)[part].at[me["mem"], at]
         return [
             remote(
-                field, field, inc_send.at[part, step - 1], inc_recv.at[part, step - 1, chunk],
+                field, field, inc_send.at[part, step - 1], inc_recv.at[step - 1, inc_sem(chunk, part)],
                 device(mem=lax.rem(me["mem"] + step, n["mem"])),
             )
             for step in range(1, n["mem"])
         ]
 
     def inc_arrivals(chunk, part):
-        at = pl.ds(chunk * per, per)
+        first, count = chunk, 1
+        if part == 0 and 0 < chunk < chunks - 1:
+            if "inner" in arrived:
+                return []
+            arrived.add("inner")
+            first, count = 1, chunks - 2
+        at = pl.ds(first * per, count * per)
         arrivals = []
         for step in range(1, n["mem"]):
             peer = lax.rem(me["mem"] + n["mem"] - step, n["mem"])
             field = (inners, rims)[part].at[peer, at]
             arrivals.append(remote(
-                field, field, inc_send.at[part, step - 1], inc_recv.at[part, step - 1, chunk], device(mem=peer)
+                field, field, inc_send.at[part, step - 1], inc_recv.at[step - 1, inc_sem(chunk, part)], device(mem=peer)
             ))
         return arrivals
+
+    arrived = set()
 
     def each(has, copies, act):
         @pl.when(has)
@@ -282,7 +299,6 @@
             stage[0, m, go], stage[1, m, go] = edges(block)
         return carry
 
-    half = chunks // 2
     tile = 2 * HALF
     loads[1].wait()
     v = vert[...].astype(F32)
@@ -461,9 +477,13 @@
     seen = {0: set(), 1: set()}
 
     def need_sides(phase, chunk):
-        wanted = (chunk, chunk + 1) if phase == 0 else (chunk - 1, chunk, chunk + 1)
+        wanted = (chunk - 1, chunk, chunk + 1)
+        if phase == 0:
+            wanted = [i for i, ks in enumerate(sets) if chunk in ks or chunk + 1 in ks]
         for k in wanted:
-            if 0 <= k < chunks + (phase == 0) and k not in seen[phase] and piece(phase, k)[1] > 0:
+            if 0 <= k < max(chunks, len(sets)) and k not in seen[phase] and piece(phase, k)[1] > 0:
+                if phase == 1 and k >= chunks:
+                    continue
                 seen[phase].add(k)
                 wait_sides(phase, *((stage, halo) if phase == 0 else (stage2, halo2)), k)
 
@@ -546,19 +566,28 @@
     with jax.named_scope("barrier"):
         pl.semaphore_wait(barrier, len(plane) + 3 * beside)
     start_inc(middle[0], 0)
-    each(has_up, row_up, "start")
     with jax.named_scope("load8"):
         loads[8].wait()
-    each(has_down, row_down, "start")
     with jax.named_scope("pack"):
         lax.fori_loop(0, groups, pack_group, 0, unroll=4)
-    for k in [*range(1, half + 1), 0, chunks - 1, chunks, *range(half + 1, chunks - 1)]:
+    waves = list(range(len(sets)))
+
+    def send_sides():
+        if not waves:
+            return
+        k = waves.pop(0)
         if piece(0, k)[1] > 0:
             for copy in side_copies(0, stage, halo, k):
                 copy.start()
-        if k == 0:
+        if sets[k] == [0]:
             each(has_up, corner_up, "start")
             each(has_down, corner_down, "start")
+
+    send_sides()
+    each(has_up, row_up, "start")
+    each(has_down, row_down, "start")
+    while waves:
+        send_sides()
     met_turns = []
 
     def meet():
@@ -579,11 +608,18 @@
     for chunk in middle[1:]:
         do_inner(chunk)
         start_inc(chunk, 0)
+        send_sides()
         if chunk == middle[half - 1]:
             meet()
+    while waves:
+        send_sides()
     with jax.named_scope("filt1"):
         near[...] = rim_matrix(taps1, taps2, 0, False)
         far[...] = rim_matrix(taps1, taps2, 1, False)
+    with jax.named_scope("squares"):
+        norms[me["mem"]] = lax.fori_loop(0, groups, squares, jnp.zeros((8, levels), F32), unroll=2)
+        for copy in norm_out:
+            copy.start()
     with jax.named_scope("load7"):
         loads[7].wait()
     last = chunks - 1
@@ -602,28 +638,28 @@
     do_end(0)
     do_rim(0)
     do_end(last)
-    with jax.named_scope("filt2"):
-        filt2[...] = full_matrix(taps1, taps2, cols, True)
     do_rim(last)
+    ahead_of = half - 1
     do_adjoint(order[0])
     if rest:
         do_rim(*rest)
     do_adjoint(order[1])
     do_rim(last - 1)
-    with jax.named_scope("squares"):
-        norms[me["mem"]] = lax.fori_loop(0, groups, squares, jnp.zeros((8, levels), F32), unroll=2)
-        for copy in norm_out:
-            copy.start()
-    at = 2
-    for position, now in enumerate(order):
-        if position < at:
-            continue
-        if position == chunks - 2:
-            while len(met_turns) <= turns:
-                meet()
+    do_adjoint(order[2])
+    do_adjoint(order[3])
+    do_adjoint(order[4])
+    with jax.named_scope("filt2"):
+        filt2[...] = full_matrix(taps1, taps2, cols, True)
+    while len(met_turns) <= turns:
+        meet()
+    done = {c: max(order.index(d) for d in (c - 1, c, c + 1)) for c in middle}
+    finals = sorted(middle, key=lambda c: (done[c], c))
+    slots = ()
+    for now in order[ahead_of + 2 :]:
         do_adjoint(now)
-    done = {c: max(order.index(d) for d in (c - 1, c, c + 1)) for c in middle}
-    for chunk in sorted(middle, key=lambda c: (done[c], c)):
+        if order.index(now) in slots:
+            do_final(finals.pop(0))
+    for chunk in finals:
         do_final(chunk)
     do_final(last)
     do_final(0)
@@ -641,13 +677,13 @@
         each(has_up, row_up + both_up + row2_up + both2_up, "wait_send")
         each(has_down, row_down + both_down + row2_down + both2_down, "wait_send")
         for phase, src, dst in ((0, stage, halo), (1, stage2, halo2)):
-            remote(src, dst.at[:, :, pl.ds(1, groups)], side_send.at[phase], side_recv.at[phase, 0], device(lon=left)).wait_send()
+            remote(src, dst.at[:, :, pl.ds(1, groups)], side_send.at[phase], side_recv.at[0], device(lon=left)).wait_send()
         for part, field in ((0, inners), (1, rims)):
             for step in range(1, n["mem"]):
                 to = lax.rem(me["mem"] + step, n["mem"])
                 whole = field.at[me["mem"]]
                 remote(
-                    whole, whole, inc_send.at[part, step - 1], inc_recv.at[part, step - 1, 0], device(mem=to)
+                    whole, whole, inc_send.at[part, step - 1], inc_recv.at[step - 1, 0], device(mem=to)
                 ).wait_send()
 
 
@@ -704,9 +740,9 @@
             pltpu.SemaphoreType.DMA((2, 2)),
             pltpu.SemaphoreType.DMA((2, 2)),
             pltpu.SemaphoreType.DMA((2,)),
-            pltpu.SemaphoreType.DMA((2, chunks + 1)),
+            pltpu.SemaphoreType.DMA((chunks // 2 + chunks + 2,)),
             pltpu.SemaphoreType.DMA((2, peers)),
-            pltpu.SemaphoreType.DMA((2, peers, chunks)),
+            pltpu.SemaphoreType.DMA((peers, chunks + 3)),
             pltpu.SemaphoreType.DMA((2,)),
             pltpu.SemaphoreType.DMA((peers,)),
             pltpu.SemaphoreType.DMA((peers,)),

time: 29.6 us -> 29 us (0.980)
  Pallas kernels: 25.1 us -> 24.5 us
    pallas_call x1, Pallas kernels: 25.1 us -> 24.5 us  [per_device(): pl.pallas_call(functools.partial(kernel, axes, sizes, entries, chunks), o...]
where the time goes in v4:
time: 29 us; the launch traced here: 28.8 us
  Pallas kernels  24.5 us (84%)
  between operations  2.33 us (8%)
  local copies, waits for them, and re-layouts  2.02 us (7%)
    pallas_call x1, Pallas kernels, per_device(): pl.pallas_call(functools.partial(kernel, axes, sizes, entries, chunks), o...  24.5 us
    unnamed x1, local copies, waits for them, and re-layouts  2.02 us

profile of v4, /device:TPU:0, one launch (start us, length us, event | category | flops | bytes accessed | tf_op | source)
XLA Modules:
  0.0 28.8 jit_solution(7063570346448006779)
XLA Ops:
  0.6 24.5 %shard_map.77 = (f32[4,64,32,128]{3,2,1,0:T(8,128)S(1)}, f32[1,1]{1,0:T(1,128)}) custom-call(f32[9]{0:T(128)} %lat_taps.1, f32[9]{0:T(128)} %lon_taps.1, bf16[4,64,32,128]{3,2,1,0:T(8,128)(2,1)} %control.1, bf16[4,64,32,128]{3,2,1,0:T(8,128)(2,1)} %ensemble.1, f32[64,32,128]{2,1,0:T(8,128)} %precision.1, bf16[128,128]{1,0:T(8,128)(2,1)} %vertical.1), custom_call_target="tpu_custom_call" | custom-call | tf_op jit(solution)/shard_map/pallas_call | solution.py:705
  25.1 2.0 %copy.10 = f32[4,64,32,128]{3,2,1,0:T(8,128)} copy(f32[4,64,32,128]{3,2,1,0:T(8,128)S(1)} %get-tuple-element.6) | data formatting | bytes 8388608

commit v5 on v4

--- a/solution.py
+++ b/solution.py
@@ -277,6 +277,7 @@
             for side in range(2):
                 two[side, :, groups + 1] = jnp.zeros((members, HALF * HALF, levels), BF16)
 
+    vert2[...] = jnp.zeros_like(vert2)
     with jax.named_scope("taps"):
         loads[4].wait()
         loads[5].wait()
@@ -300,9 +301,6 @@
         return carry
 
     tile = 2 * HALF
-    loads[1].wait()
-    v = vert[...].astype(F32)
-    vt = v.T
     blank = jnp.zeros((levels, levels), F32)
 
     def diagonal(block):
@@ -312,8 +310,6 @@
             [jnp.concatenate([block, blank], axis=1), jnp.concatenate([blank, block], axis=1)], axis=0
         ).astype(BF16)
 
-    vert2[...] = diagonal(v)
-    vert2t[...] = diagonal(vt)
     sums[...] = jnp.zeros_like(sums)
 
     def tile_sum(x):
@@ -559,6 +555,10 @@
 
     middle = list(range(1, chunks - 1))
     turns = n["lat"] - 1
+    with jax.named_scope("load1"):
+        loads[1].wait()
+    for j in range(width):
+        vert2[j * levels : (j + 1) * levels, j * levels : (j + 1) * levels] = vert[...]
     with jax.named_scope("load0"):
         loads[0].wait()
         loads[2].wait()
@@ -614,6 +614,7 @@
     while waves:
         send_sides()
     with jax.named_scope("filt1"):
+        vert2t[...] = diagonal(vert[...].astype(F32).T)
         near[...] = rim_matrix(taps1, taps2, 0, False)
         far[...] = rim_matrix(taps1, taps2, 1, False)
     with jax.named_scope("squares"):
@@ -661,8 +662,9 @@
             do_final(finals.pop(0))
     for chunk in finals:
         do_final(chunk)
+        if chunk == 1:
+            do_final(0)
     do_final(last)
-    do_final(0)
 
     with jax.named_scope("redend"):
         if across:

time: 29 us -> 29 us (level)
  no operation moved by 1% of the time
where the time goes in v5:
time: 29 us; the launch traced here: 28.8 us
  Pallas kernels  24.5 us (84%)
  between operations  2.33 us (8%)
  local copies, waits for them, and re-layouts  2.02 us (7%)
    pallas_call x1, Pallas kernels, per_device(): pl.pallas_call(functools.partial(kernel, axes, sizes, entries, chunks), o...  24.5 us
    unnamed x1, local copies, waits for them, and re-layouts  2.02 us

profile of v5, /device:TPU:0, one launch (start us, length us, event | category | flops | bytes accessed | tf_op | source)
XLA Modules:
  0.0 28.8 jit_solution(12163403256293470444)
XLA Ops:
  0.6 24.5 %shard_map.77 = (f32[4,64,32,128]{3,2,1,0:T(8,128)S(1)}, f32[1,1]{1,0:T(1,128)}) custom-call(f32[9]{0:T(128)} %lat_taps.1, f32[9]{0:T(128)} %lon_taps.1, bf16[4,64,32,128]{3,2,1,0:T(8,128)(2,1)} %control.1, bf16[4,64,32,128]{3,2,1,0:T(8,128)(2,1)} %ensemble.1, f32[64,32,128]{2,1,0:T(8,128)} %precision.1, bf16[128,128]{1,0:T(8,128)(2,1)} %vertical.1), custom_call_target="tpu_custom_call" | custom-call | tf_op jit(solution)/shard_map/pallas_call | solution.py:707
  25.1 2.0 %copy.10 = f32[4,64,32,128]{3,2,1,0:T(8,128)} copy(f32[4,64,32,128]{3,2,1,0:T(8,128)S(1)} %get-tuple-element.6) | data formatting | bytes 8388608
